TPU v7x, 32 devices: a whole 2x2x4 slice. The times are simulated.
32 devices in a mesh: dp: 8 (over y, x, core), mp: 4 (over z).
Axes of the slice: x: 2, y: 2, z: 4, core: 2. Of those that a mesh axis runs over, the one named last changes fastest.
Arguments:
- layer_input: bfloat16 [6464, 768], P(('dp', 'mp')), may hold values from -6 to 6
- lengths: int32 [32], P('dp'), may hold values from 10 to 202, as said below
- ln1_gain: float32 [768], replicated, may hold values from 0.5 to 1.5
- ln1_bias: float32 [768], replicated, may hold values from -1.25 to 1.25
- w_qkv: bfloat16 [768, 2304], P(None, 'mp'), may hold values from -0.21875 to 0.21875
- b_qkv: float32 [2304], P('mp'), may hold values from -1.25 to 1.25
- features: float32 [12, 64, 32], P('mp'), may hold values from -6 to 6
- w_out: bfloat16 [768, 768], P('mp'), may hold values from -1.75 to 1.75
- b_out: float32 [768], replicated, may hold values from -1.25 to 1.25
- ln2_gain: float32 [768], replicated, may hold values from 0.5 to 1.5
- ln2_bias: float32 [768], replicated, may hold values from -1.25 to 1.25
- w_up: bfloat16 [768, 3072], P(None, 'mp'), may hold values from -0.21875 to 0.21875
- b_up: float32 [3072], P('mp'), may hold values from -1.25 to 1.25
- w_down: bfloat16 [3072, 768], P('mp'), may hold values from -0.109375 to 0.109375
- b_down: float32 [768], replicated, may hold values from -1.25 to 1.25
- cotangent: bfloat16 [6464, 768], P(('dp', 'mp')), may hold values from -6 to 6
Outputs:
- layer_output: bfloat16 [6464, 768], P(('dp', 'mp'))
- grad_x: float32 [6464, 768], P(('dp', 'mp'))
- grad_ln1_gain: float32 [768], replicated
- grad_ln1_bias: float32 [768], replicated
- grad_w_qkv: float32 [768, 2304], P('dp', 'mp')
- grad_b_qkv: float32 [2304], P('mp')
- grad_w_out: float32 [768, 768], P('mp', 'dp')
- grad_b_out: float32 [768], replicated
- grad_ln2_gain: float32 [768], replicated
- grad_ln2_bias: float32 [768], replicated
- grad_w_up: float32 [768, 3072], P('dp', 'mp')
- grad_b_up: float32 [3072], P('mp')
- grad_w_down: float32 [3072, 768], P('mp', 'dp')
- grad_b_down: float32 [768], replicated
Inputs may be any that keep to these rules, and one draw needn't show every extreme that they name: A molecule's live tokens are the first lengths[m] of its 202 slots; some molecule has exactly 202 and some exactly 10.
All inputs are finite; a program needn't handle non-finite values.
Results may differ from a plain program's by a relative error of at most 0.02.
Values may be sent and summed in bfloat16 or wider, within the bound.
A program may use at most 128 MiB of HBM per device.

v0:
```python
import jax
import jax.numpy as jnp
from jax import lax
from jax.sharding import PartitionSpec as P

MAXLEN = 202


EPSILON = 1e-05


def norm_rows(values, gain, shift):
    centred = values - jnp.mean(values, axis=-1, keepdims=True)
    factor = lax.rsqrt(jnp.mean(centred * centred, axis=-1, keepdims=True) + EPSILON)
    normed = centred * factor
    return (normed * gain + shift, normed, factor)


def norm_back(grad_norm, normed, factor, gain):
    grad_hat = grad_norm * gain
    inner = (
        grad_hat
        - jnp.mean(grad_hat, axis=-1, keepdims=True)
        - normed * jnp.mean(grad_hat * normed, axis=-1, keepdims=True)
    )
    return (factor * inner, jnp.sum(grad_norm * normed, axis=0), jnp.sum(grad_norm, axis=0))


def rotate(values, positions):
    half = values.shape[-1] // 2
    freq = 10000.0 ** (-jnp.arange(half, dtype=jnp.float32) * 2.0 / values.shape[-1])
    angle = positions.astype(jnp.float32)[:, None] * freq[None, :]
    cosine = jnp.concatenate([jnp.cos(angle), jnp.cos(angle)], axis=-1)[:, None, :]
    sine = jnp.concatenate([jnp.sin(angle), jnp.sin(angle)], axis=-1)[:, None, :]
    turned = jnp.concatenate([-values[..., half:], values[..., :half]], axis=-1)
    return values * cosine + turned * sine


def featurize(projected, features, positions):
    heads = features.shape[0]
    head_size = features.shape[1]
    blocks = projected.reshape(projected.shape[0], heads, 3, head_size)
    factor = head_size ** (-0.25)
    query = rotate(blocks[:, :, 0], positions) * factor
    keyed = rotate(blocks[:, :, 1], positions) * factor
    map_q = (
        jax.nn.elu(jnp.einsum("ghe,hef->ghf", query, features, precision=lax.Precision.HIGHEST))
        + 1.0
    )
    map_k = (
        jax.nn.elu(jnp.einsum("ghe,hef->ghf", keyed, features, precision=lax.Precision.HIGHEST))
        + 1.0
    )
    return (map_q, map_k, blocks[:, :, 2])


def core(map_q, map_k, column_block, key_mask, molecules):
    total_rows, heads, feats = map_q.shape
    head_size = column_block.shape[-1]
    span = total_rows // molecules
    query_maps = map_q.reshape(molecules, span, heads, feats)
    key_maps = (map_k * key_mask[:, None, None]).reshape(molecules, span, heads, feats)
    values_four = column_block.reshape(molecules, span, heads, head_size)
    state = jnp.einsum("mlhf,mlhe->mhfe", key_maps, values_four, precision=lax.Precision.HIGHEST)
    summed = jnp.sum(key_maps, axis=1)
    numer = jnp.einsum("mlhf,mhfe->mlhe", query_maps, state, precision=lax.Precision.HIGHEST)
    denom = jnp.einsum("mlhf,mhf->mlh", query_maps, summed, precision=lax.Precision.HIGHEST)
    return (numer / denom[..., None]).reshape(total_rows, heads * head_size)


def gelu_exact(argument):
    return jax.nn.gelu(argument, approximate=False)


def contract_last(left, right):
    return lax.dot_general(
        left, right, (((1,), (1,)), ((), ())), preferred_element_type=jnp.float32
    )


def contract_first(left, right):
    return lax.dot_general(
        left, right, (((0,), (0,)), ((), ())), preferred_element_type=jnp.float32
    )


def slot_masks(counts):
    slot_index = jnp.arange(MAXLEN, dtype=jnp.int32)
    number = counts.shape[0]
    mask_rows = (slot_index[None, :] < counts[:, None]).astype(jnp.float32).reshape(number * MAXLEN)
    return (mask_rows, jnp.tile(slot_index, number))


def local(
    layer_input,
    lengths,
    ln1_gain,
    ln1_bias,
    w_qkv,
    b_qkv,
    features,
    w_out,
    b_out,
    ln2_gain,
    ln2_bias,
    w_up,
    b_up,
    w_down,
    b_down,
    cotangent,
):
    inputs = layer_input.astype(jnp.float32)
    normed_one, hat_one, factor_one = norm_rows(inputs, ln1_gain, ln1_bias)
    first_local = normed_one.astype(jnp.bfloat16)
    qkv_matrix, out_matrix, qkv_bias, feature_set = (w_qkv, w_out, b_qkv, features)
    attn_mask, attn_positions = slot_masks(lengths)
    attn_molecules = lengths.shape[0]
    first_rows = lax.all_gather(first_local, "mp", axis=0, tiled=True)
    projected = jnp.dot(first_rows, qkv_matrix, preferred_element_type=jnp.float32) + qkv_bias
    feature_out, feature_pull = jax.vjp(
        lambda argument: featurize(argument, feature_set, attn_positions), projected
    )
    widened = tuple((member.astype(jnp.bfloat16).astype(jnp.float32) for member in feature_out))
    attended, core_pull = jax.vjp(
        lambda query_map, key_map, column_block: core(
            query_map, key_map, column_block, attn_mask, attn_molecules
        ),
        *widened
    )
    mixed = attended.astype(jnp.bfloat16)
    middle = (
        inputs
        + lax.psum_scatter(
            jnp.dot(mixed, w_out, preferred_element_type=jnp.float32).astype(jnp.bfloat16),
            "mp",
            scatter_dimension=0,
            tiled=True,
        ).astype(jnp.float32)
        + b_out
    )
    normed_two, hat_two, factor_two = norm_rows(middle, ln2_gain, ln2_bias)
    second = normed_two.astype(jnp.bfloat16)
    second_rows = lax.all_gather(second, "mp", axis=0, tiled=True)
    pre_act = jnp.dot(second_rows, w_up, preferred_element_type=jnp.float32) + b_up
    activated, gelu_pull = jax.vjp(gelu_exact, pre_act)
    hidden = activated.astype(jnp.bfloat16)
    ffn_branch = (
        lax.psum_scatter(
            jnp.dot(hidden, w_down, preferred_element_type=jnp.float32).astype(jnp.bfloat16),
            "mp",
            scatter_dimension=0,
            tiled=True,
        ).astype(jnp.float32)
        + b_down
    )
    outputs = (middle + ffn_branch).astype(jnp.bfloat16)
    grad_output = cotangent.astype(jnp.float32)
    grad_b_down = jnp.sum(grad_output, axis=0)
    grad_rows = lax.all_gather(cotangent, "mp", axis=0, tiled=True)
    grad_hidden = contract_last(grad_rows, w_down)
    grad_pre = gelu_pull(grad_hidden)[0].astype(jnp.bfloat16)
    grad_w_down = contract_first(hidden, grad_rows)
    grad_w_up = contract_first(second_rows, grad_pre)
    grad_b_up = jnp.sum(grad_pre.astype(jnp.float32), axis=0)
    grad_second = lax.psum_scatter(
        contract_last(grad_pre, w_up).astype(jnp.bfloat16), "mp", scatter_dimension=0, tiled=True
    ).astype(jnp.float32)
    grad_mid_norm, grad_ln2_gain, grad_ln2_bias = norm_back(
        grad_second, hat_two, factor_two, ln2_gain
    )
    grad_middle = grad_output + grad_mid_norm
    grad_branch = grad_middle.astype(jnp.bfloat16)
    grad_b_out = jnp.sum(grad_branch.astype(jnp.float32), axis=0)
    branch_rows = lax.all_gather(grad_branch, "mp", axis=0, tiled=True)
    grad_mixed = contract_last(branch_rows, out_matrix)
    out_part = contract_first(mixed, branch_rows)
    grad_maps = core_pull(grad_mixed)
    grad_projected = feature_pull(grad_maps)[0].astype(jnp.bfloat16)
    qkv_bias_part = jnp.sum(grad_projected.astype(jnp.float32), axis=0)
    qkv_part = contract_first(first_rows, grad_projected)
    grad_w_qkv, grad_b_qkv, grad_w_out = (qkv_part, qkv_bias_part, out_part)
    grad_first = lax.psum_scatter(
        contract_last(grad_projected, w_qkv).astype(jnp.bfloat16),
        "mp",
        scatter_dimension=0,
        tiled=True,
    ).astype(jnp.float32)
    grad_in_norm, grad_ln1_gain, grad_ln1_bias = norm_back(
        grad_first, hat_one, factor_one, ln1_gain
    )
    grad_inputs = grad_middle + grad_in_norm
    grad_w_qkv, grad_w_out, grad_w_up, grad_w_down = (
        lax.psum_scatter(grad_w_qkv, "dp", scatter_dimension=0, tiled=True),
        lax.psum_scatter(grad_w_out, "dp", scatter_dimension=1, tiled=True),
        lax.psum_scatter(grad_w_up, "dp", scatter_dimension=0, tiled=True),
        lax.psum_scatter(grad_w_down, "dp", scatter_dimension=1, tiled=True),
    )
    grad_b_qkv, grad_b_up = lax.psum((grad_b_qkv, grad_b_up), "dp")
    summed_small = lax.psum(
        (grad_ln1_gain, grad_ln1_bias, grad_b_out, grad_ln2_gain, grad_ln2_bias, grad_b_down),
        ("dp", "mp"),
    )
    return (
        outputs,
        grad_inputs,
        summed_small[0],
        summed_small[1],
        grad_w_qkv,
        grad_b_qkv,
        grad_w_out,
        summed_small[2],
        summed_small[3],
        summed_small[4],
        grad_w_up,
        grad_b_up,
        grad_w_down,
        summed_small[5],
    )


def solution(mesh):
    placed = (
        P(("dp", "mp"), None),
        P("dp"),
        P(),
        P(),
        P(None, "mp"),
        P("mp"),
        P("mp", None, None),
        P("mp", None),
        P(),
        P(),
        P(),
        P(None, "mp"),
        P("mp"),
        P("mp", None),
        P(),
        P(("dp", "mp"), None),
    )
    return jax.shard_map(
        local,
        mesh=mesh,
        in_specs=placed,
        out_specs=(
            P(("dp", "mp"), None),
            P(("dp", "mp"), None),
            P(),
            P(),
            P("dp", "mp"),
            P("mp"),
            P("mp", "dp"),
            P(),
            P(),
            P(),
            P("dp", "mp"),
            P("mp"),
            P("mp", "dp"),
            P(),
        ),
        check_vma=False,
    )
```

profile of v0, /device:TPU:0, one launch (start us, length us, event | category | flops | bytes accessed | tf_op | source)
XLA Modules:
  0.0 409.1 jit_solution(9099996804335391851)
XLA Ops:
  9.7 1.9 fusion.91
  14.7 31.8 %all-gather.9.cloned.1.call-done = bf16[4,202,768]{2,1,0:T(8,128)(2,1)} async-done(((bf16[1,202,768]{2,1,0:T(8,128)(2,1)}), bf16[4,202,768]{2,1,0:T(8,128)(2,1)}) %all-gather.9.cloned.1.call-update) | async-done | bytes 1241104 | tf_op jit(solution)/shard_map/all_gather | solution.py:118
  46.5 1.6 reshape.154
  48.1 2.7 convolution_add_fusion
  54.2 1.6 fusion.72
  55.8 1.8 reshape.147
  58.7 1.6 convert_multiply_fusion.4
  63.6 2.4 divide_convert_fusion
  66.6 1.6 convolution_convert_fusion.2
  68.3 32.9 %fusion = bf16[208,768]{1,0:T(8,128)(2,1)} fusion(bf16[808,768]{1,0:T(8,128)(2,1)S(1)} %convolution_convert_fusion.2), kind=kCustom, calls=%all-reduce-scatter | all-reduce-scatter fusion | flops 638977 | bytes 1561088
  104.8 2.0 concatenate.18
  107.4 1.7 fusion.90
  109.4 2.7 reshape.158
  112.1 30.2 %all-gather.11.cloned.1.call-done = bf16[4,202,768]{2,1,0:T(8,128)(2,1)} async-done(((bf16[1,202,768]{2,1,0:T(8,128)(2,1)}), bf16[4,202,768]{2,1,0:T(8,128)(2,1)}) %all-gather.11.cloned.1.call-update) | async-done | bytes 1241104 | tf_op jit(solution)/shard_map/all_gather | solution.py:143
  142.3 1.6 reshape.156
  144.0 2.9 fusion.115
  146.9 8.4 %convert_reduce_fusion = (f32[768]{0:T(1024)}, bf16[808,768]{1,0:T(8,128)(2,1)S(1)}, f32[808,768]{1,0:T(8,128)}) fusion(f32[808,768]{1,0:T(8,128)S(1)} %fusion.115, f32[768]{0:T(1024)S(1)} %copy-done.41, bf16[808,768]{1,0:T(8,128)(2,1)S(1)} %copy-done.13, bf16[768,768]{1,0:T(8,128)(2,1)S(1)} %copy-done), kind=kOutput, calls=%fused_computation.2 | convolution fusion | flops 999695616 | bytes 8632320 | tf_op jit(solution)/shard_map/dot_general | solution.py:76
  156.4 2.3 convolution_convert_fusion
  158.7 28.5 %fusion.2 = bf16[208,768]{1,0:T(8,128)(2,1)S(1)} fusion(bf16[808,768]{1,0:T(8,128)(2,1)} %convolution_convert_fusion), kind=kCustom, calls=%all-reduce-scatter.2 | all-reduce-scatter fusion | flops 638977 | bytes 1561088
  187.3 1.6 collective-permute-start.2
  188.9 1.6 collective-permute-done.2
  192.1 2.1 convert_reduce_fusion.6
  195.1 31.9 %all-gather.15.cloned.1.call-done = bf16[4,202,768]{2,1,0:T(8,128)(2,1)} async-done(((bf16[1,202,768]{2,1,0:T(8,128)(2,1)}), bf16[4,202,768]{2,1,0:T(8,128)(2,1)}) %all-gather.15.cloned.1.call-update) | async-done | bytes 1241104 | tf_op jit(solution)/shard_map/all_gather | solution.py:174
  227.0 1.6 reshape.160
  228.7 2.6 convolution_bitcast_fusion
  231.4 2.9 multiply_convert_fusion
  235.4 2.9 fusion.119
  238.3 1.5 copy.85
  240.5 4.6 %fusion.118 = f32[768,768]{1,0:T(8,128)} fusion(bf16[808,768]{1,0:T(8,128)(2,1)} %copy-done.12, bf16[808,768]{1,0:T(8,128)(2,1)} %copy-done.47), kind=kOutput, calls=%fused_computation.196 | convolution fusion | flops 953155584 | bytes 4841472 | tf_op jit(solution)/shard_map/dot_general | solution.py:82
  245.4 2.5 fusion.116
  247.8 1.8 reshape.148
  249.6 1.4 multiply_reduce_fusion
  252.8 2.0 reshape.151
  256.0 1.5 fusion.19
  259.4 1.7 convolution_bitcast_fusion.1
  262.2 1.9 fusion.59
  264.2 1.9 fusion.61
  268.5 2.7 fusion.117
  271.3 2.2 convolution_convert_fusion.1
  273.5 2.3 convolution_convert_fusion.3
  275.8 47.7 %fusion.110 = (bf16[208,768]{1,0:T(8,128)(2,1)S(1)}, bf16[208,768]{1,0:T(8,128)(2,1)S(1)}) fusion(bf16[808,768]{1,0:T(8,128)(2,1)} %convolution_convert_fusion.1, bf16[808,768]{1,0:T(8,128)(2,1)} %convolution_convert_fusion.3), kind=kCustom, calls=%all-reduce-scatter.4 | all-reduce-scatter fusion | flops 1277953 | bytes 3121664
  323.6 2.6 collective-permute-start.3
  326.8 2.6 collective-permute-start.1
  329.6 13.6 %all-reduce.16 = (f32[576]{0:T(1024)}, f32[768]{0:T(1024)}) all-reduce(f32[576]{0:T(1024)S(1)} %reduce_sum.181, f32[768]{0:T(1024)S(1)} %copy-done.42), channel_id=1, replica_groups=mesh['dp'=8,'mp'=4] {'dp'}, use_global_device_ids=true, to_apply=%region_20.21 | all-reduce | flops 1344 | bytes 10752 | tf_op jit(solution)/shard_map/psum | solution.py:198
  345.2 38.1 %all-reduce.15 = (f32[768]{0:T(1024)}, f32[768]{0:T(1024)}, f32[768]{0:T(1024)}, f32[768]{0:T(1024)}, f32[768]{0:T(1024)}, /*index=5*/f32[768]{0:T(1024)}) all-reduce(f32[768]{0:T(1024)S(1)} %get-tuple-element.16, f32[768]{0:T(1024)S(1)} %get-tuple-element.21, ...), channel_id=1, replica_groups=mesh['dp'=8,'mp'=4] {'dp','mp'}, use_global_device_ids=true, to_apply=%region_15.16 | all-reduce | flops 4608 | bytes 36864 | tf_op jit(solution)/shard_map/psum | solution.py:199
  383.3 2.1 fusion.45
  385.4 1.6 copy.94
  387.1 15.2 %reduce-scatter.15.cloned.1.call-done = f32[96,576]{1,0:T(8,128)} async-done(((f32[768,576]{1,0:T(8,128)}), f32[96,576]{1,0:T(8,128)}) %reduce-scatter.15.cloned.1.call-update) | async-done | bytes 221200 | tf_op jit(solution)/shard_map/reduce_scatter | solution.py:193
  (184 shorter events, 34.2 us)
Async XLA Ops:
  7.2 139.7 %copy-start = (bf16[768,768]{1,0:T(8,128)(2,1)S(1)}, bf16[768,768]{1,0:T(8,128)(2,1)}, u32[]{:S(2)}) copy-start(bf16[768,768]{1,0:T(8,128)(2,1)} %param.29) | copy-start | bytes 3538948
  7.2 39.3 %all-gather.9.cloned.1.call-start = ((), (), s32[]{:S(2)}) async-start(), calls=%async_computation.7 | async-start | bytes 1597440 | tf_op jit(solution)/shard_map/all_gather | solution.py:118
  8.4 4.9 %copy-start.29 = (f32[202]{0:T(256)}, f32[202]{0:T(256)S(1)}, u32[]{:S(2)}) copy-start(f32[202]{0:T(256)S(1)} %broadcast_multiply_fusion.7) | copy-start | bytes 2428
  9.7 3.6 copy-start.33
  9.7 38.5 %copy-start.46 = (f32[576]{0:T(1024)S(1)}, f32[576]{0:T(1024)}, u32[]{:S(2)}) copy-start(f32[576]{0:T(1024)} %param.21) | copy-start | bytes 6916
  11.7 97.7 %all-gather.13.cloned.1.call-start = ((), (), s32[]{:S(2)}) async-start(), calls=%async_computation.9 | async-start | bytes 1597440 | tf_op jit(solution)/shard_map/all_gather | solution.py:159
  12.4 129.9 %all-gather.11.cloned.1.call-start = ((), (), s32[]{:S(2)}) async-start(), calls=%async_computation.8 | async-start | bytes 1597440 | tf_op jit(solution)/shard_map/all_gather | solution.py:143
  13.3 45.4 %copy-start.27 = (f32[808]{0:T(1024)}, f32[808]{0:T(1024)S(1)}, u32[]{:S(2)}) copy-start(f32[808]{0:T(1024)S(1)} %reshape.152) | copy-start | bytes 9700
  53.1 9.9 %copy-start.4 = (bf16[4,202,3,64]{1,0,3,2:T(4,128)(2,1)}, bf16[4,202,3,64]{1,0,3,2:T(4,128)(2,1)S(1)}, u32[]{:S(2)}) copy-start(bf16[4,202,3,64]{1,0,3,2:T(4,128)(2,1)S(1)} %convert_element_type.128) | copy-start | bytes 930820
  61.8 4.1 %copy-start.21 = (f32[4,3,32]{0,2,1:T(8,128)}, f32[4,3,32]{0,2,1:T(8,128)S(1)}, u32[]{:S(2)}) copy-start(f32[4,3,32]{0,2,1:T(8,128)S(1)} %reduce_sum.170) | copy-start | bytes 4612
  63.1 2.9 copy-start.36
  66.0 37.2 %copy-start.43 = (u32[32]{0:T(128)S(1)}, u32[32]{0:T(128)}, u32[]{:S(2)}) copy-start(u32[32]{0:T(128)} %constant.120) | copy-start | bytes 388
  66.3 40.5 %copy-start.1 = (bf16[202,768]{1,0:T(8,128)(2,1)S(1)}, bf16[202,768]{1,0:T(8,128)(2,1)}, u32[]{:S(2)}) copy-start(bf16[202,768]{1,0:T(8,128)(2,1)} %param.16) | copy-start | bytes 930820
  66.3 40.5 %copy-start.24 = (f32[768]{0:T(1024)S(1)}, f32[768]{0:T(1024)}, u32[]{:S(2)}) copy-start(f32[768]{0:T(1024)} %param.24) | copy-start | bytes 9220
  66.6 37.8 %copy-start.6 = (bf16[808,192]{0,1:T(8,128)(2,1)}, bf16[808,192]{0,1:T(8,128)(2,1)S(1)}, u32[]{:S(2)}) copy-start(bf16[808,192]{0,1:T(8,128)(2,1)S(1)} %convert_element_type.131) | copy-start | bytes 930820
  101.9 2.9 collective-permute-start
  107.0 5.0 %copy-start.31 = (f32[202]{0:T(256)}, f32[202]{0:T(256)S(1)}, u32[]{:S(2)}) copy-start(f32[202]{0:T(256)S(1)} %broadcast_multiply_fusion.6) | copy-start | bytes 2428
  107.4 4.7 %copy-start.38 = (f32[202]{0:T(256)}, f32[202]{0:T(256)S(1)}, u32[]{:S(2)}) copy-start(f32[202]{0:T(256)S(1)} %add_rsqrt_fusion) | copy-start | bytes 2428
  109.1 117.9 %all-gather.15.cloned.1.call-start = ((), (), s32[]{:S(2)}) async-start(), calls=%async_computation.10 | async-start | bytes 1597440 | tf_op jit(solution)/shard_map/all_gather | solution.py:174
  143.9 2.9 copy-start.12
  143.9 2.9 copy-start.13
  143.9 2.9 copy-start.41
  146.9 8.4 %copy-start.7 = (f32[808,768]{1,0:T(8,128)}, f32[808,768]{1,0:T(8,128)S(1)}, u32[]{:S(2)}) copy-start(f32[808,768]{1,0:T(8,128)S(1)} %fusion.115) | copy-start | bytes 7446532
  146.9 9.5 %copy-start.44 = (bf16[768,768]{1,0:T(8,128)(2,1)S(1)}, bf16[768,768]{1,0:T(8,128)(2,1)}, u32[]{:S(2)}) copy-start(bf16[768,768]{1,0:T(8,128)(2,1)} %param.27) | copy-start | bytes 3538948
  156.4 34.5 %copy-start.25 = (f32[768]{0:T(1024)S(1)}, f32[768]{0:T(1024)}, u32[]{:S(2)}) copy-start(f32[768]{0:T(1024)} %param.25) | copy-start | bytes 9220
  156.4 34.5 %copy-start.32 = (f32[202]{0:T(256)S(1)}, f32[202]{0:T(256)}, u32[]{:S(2)}) copy-start(f32[202]{0:T(256)} %copy-done.31) | copy-start | bytes 2428
  156.4 34.6 %copy-start.39 = (f32[202]{0:T(256)S(1)}, f32[202]{0:T(256)}, u32[]{:S(2)}) copy-start(f32[202]{0:T(256)} %copy-done.38) | copy-start | bytes 2428
  187.3 3.2 collective-permute-start.2
  195.0 190.4 %reduce-scatter.21.cloned.1.call-start = ((), (), s32[]{:S(2)}) async-start(), calls=%async_computation.11 | async-start | bytes 884736
  231.3 155.8 %reduce-scatter.19.cloned.1.call-start = ((), (), s32[]{:S(2)}) async-start(), calls=%async_computation.6 | async-start | bytes 2654208 | tf_op jit(solution)/shard_map/reduce_scatter | solution.py:196
  231.4 4.0 copy-start.14
  238.3 148.8 %reduce-scatter.17.cloned.1.call-start = ((), (), s32[]{:S(2)}) async-start(), calls=%async_computation.5 | async-start | bytes 2654208 | tf_op jit(solution)/shard_map/reduce_scatter | solution.py:195
  245.1 6.0 %copy-start.40 = (f32[4,3,32]{2,1,0:T(4,128)S(1)}, f32[4,3,32]{2,1,0:T(4,128)}, u32[]{:S(2)}) copy-start(f32[4,3,32]{2,1,0:T(4,128)} %copy.85) | copy-start | bytes 4612
  245.1 157.2 %reduce-scatter.15.cloned.1.call-start = ((), (), s32[]{:S(2)}) async-start(), calls=%async_computation.4 | async-start | bytes 2211840 | tf_op jit(solution)/shard_map/reduce_scatter | solution.py:193
  247.8 3.3 copy-start.23
  247.8 3.3 copy-start.37
  251.8 5.7 %copy-start.5 = (bf16[4,202,3,64]{1,0,3,2:T(4,128)(2,1)S(1)}, bf16[4,202,3,64]{1,0,3,2:T(4,128)(2,1)}, u32[]{:S(2)}) copy-start(bf16[4,202,3,64]{1,0,3,2:T(4,128)(2,1)} %copy-done.4) | copy-start | bytes 930820
  261.2 3.0 copy-start.28
  262.2 3.8 copy-start.17
  268.5 2.8 copy-start.11
  275.8 53.8 %copy-start.42 = (f32[768]{0:T(1024)S(1)}, f32[768]{0:T(1024)}, u32[]{:S(2)}) copy-start(f32[768]{0:T(1024)} %get-tuple-element.34) | copy-start | bytes 9220
  275.8 68.9 %copy-start.26 = (f32[768]{0:T(1024)S(1)}, f32[768]{0:T(1024)}, u32[]{:S(2)}) copy-start(f32[768]{0:T(1024)} %param.18) | copy-start | bytes 9220
  275.8 68.9 %copy-start.30 = (f32[202]{0:T(256)S(1)}, f32[202]{0:T(256)}, u32[]{:S(2)}) copy-start(f32[202]{0:T(256)} %copy-done.29) | copy-start | bytes 2428
  275.8 68.9 %copy-start.34 = (f32[202]{0:T(256)S(1)}, f32[202]{0:T(256)}, u32[]{:S(2)}) copy-start(f32[202]{0:T(256)} %copy-done.33) | copy-start | bytes 2428
  275.8 69.4 %copy-start.35 = (f32[768]{0:T(1024)S(1)}, f32[768]{0:T(1024)}, u32[]{:S(2)}) copy-start(f32[768]{0:T(1024)} %get-tuple-element.14) | copy-start | bytes 9220
  275.8 107.5 %copy-start.3 = (f32[202,768]{1,0:T(8,128)S(1)}, f32[202,768]{1,0:T(8,128)}, u32[]{:S(2)}) copy-start(f32[202,768]{1,0:T(8,128)} %copy-done.2) | copy-start | bytes 1861636
  323.6 19.5 %collective-permute-start.3 = (bf16[18,768]{1,0:T(8,128)(2,1)S(1)}, bf16[18,768]{1,0:T(8,128)(2,1)S(1)}, u32[]{:S(2)}, u32[]{:S(2)}) collective-permute-start(bf16[18,768]{1,0:T(8,128)(2,1)S(1)} %slice.39), channel_id=1, source_target_pairs={{0,1},{1,2},{2,3},{4,5},{5,6},{6,7},{8,9},{9,10},{10,11},{12,13},{... | collective-permute-start | bytes 82952
  326.8 16.7 %collective-permute-start.1 = (bf16[18,768]{1,0:T(8,128)(2,1)}, bf16[18,768]{1,0:T(8,128)(2,1)}, u32[]{:S(2)}, u32[]{:S(2)}) collective-permute-start(bf16[18,768]{1,0:T(8,128)(2,1)} %slice.37), channel_id=1, source_target_pairs={{0,1},{1,2},{2,3},{4,5},{5,6},{6,7},{8,9},{9,10},{10,11},{12,13},{... | collective-permute-start | bytes 82952
  (12 other events, 19.1 us)
Sparse Core Ops, SparseCore 0:
  11.8 34.6 all-gather.8
  48.1 36.3 all-gather.12
  109.2 33.0 all-gather.10
  195.1 31.8 all-gather.14
  231.4 34.0 reduce-scatter.20
  269.3 42.3 reduce-scatter.18
  315.6 42.4 reduce-scatter.16
  362.1 40.1 reduce-scatter.14
where the time goes:
time: 411 us; the launch traced here: 409 us
  blocking collectives  161 us (39%)
  waiting for transfers between devices  112 us (27%)
  matrix products  54.1 us (13%)
  local copies, waits for them, and re-layouts  35.5 us (9%)
  other arithmetic  22.2 us (5%)
  between operations  15.7 us (4%)
  starting transfers between devices  8.88 us (2%)
    unnamed x3, blocking collectives  109 us
    psum x1, blocking collectives, local(): lax.psum((grad_ln1_gain, grad_ln1_bias, grad_b_out, grad_ln2_gain, grad_l...  38.1 us
    all_gather x1, waiting for transfers between devices, local(): branch_rows = lax.all_gather(grad_branch, 'mp', axis=0, tiled=True)  31.9 us
    all_gather x1, waiting for transfers between devices, local(): first_rows = lax.all_gather(first_local, 'mp', axis=0, tiled=True)  31.8 us
    all_gather x1, waiting for transfers between devices, local(): second_rows = lax.all_gather(second, 'mp', axis=0, tiled=True)  30.2 us
    unnamed x111, local copies, waits for them, and re-layouts  20.4 us
    dot_general x4, matrix products, contract_last(): lax.dot_general(left, right, (((1,), (1,)), ((), ())), preferred_element_...  15.5 us
    reduce_scatter x1, waiting for transfers between devices, local(): lax.psum_scatter(grad_w_qkv, 'dp', scatter_dimension=0, tiled=True)  15.2 us
  transfers between devices with their start and end apart: 12, of which 6 were waited for; matrix products, arithmetic and copies ran while one was open for 39% of the time, Pallas kernels for 0%

commit v1 on v0

v1 whole, which is shorter than its diff:
```python
import functools

import jax
import jax.numpy as jnp
import numpy as np
from jax import lax
from jax.experimental import pallas as pl
from jax.experimental.pallas import tpu as pltpu
from jax.sharding import PartitionSpec as P

MESH = pl.DeviceIdType.MESH
BF16 = jnp.bfloat16
F32 = jnp.float32
EPSILON = 1e-05
GROUP = 8


def dot_nn(left, right):
    return lax.dot_general(left, right, (((1,), (0,)), ((), ())), preferred_element_type=F32)


def dot_nt(left, right):
    return lax.dot_general(left, right, (((1,), (1,)), ((), ())), preferred_element_type=F32)


def dot_tn(left, right):
    return lax.dot_general(left, right, (((0,), (0,)), ((), ())), preferred_element_type=F32)


def split(values):
    high = values.astype(BF16)
    return high, (values - high.astype(F32)).astype(BF16)


def normalize(values):
    centred = values - jnp.mean(values, axis=-1, keepdims=True)
    factor = lax.rsqrt(jnp.mean(centred * centred, axis=-1, keepdims=True) + EPSILON)
    return centred * factor, factor


def norm_back(grad, gain, normed, factor):
    hat = grad * gain
    return factor * (
        hat
        - jnp.mean(hat, axis=-1, keepdims=True)
        - normed * jnp.mean(hat * normed, axis=-1, keepdims=True)
    )


def column_sum(values):
    return jnp.sum(values, axis=0, keepdims=True)


def swap_halves(values):
    width = values.shape[1]
    lane = lax.broadcasted_iota(jnp.int32, values.shape, 1)
    return jnp.where(lane % 64 < 32, pltpu.roll(values, width - 32, 1), pltpu.roll(values, 32, 1))


def layer_kernel(live, *refs):
    (
        x_ref, c_ref, len_ref, vec_ref, feat_ref, trig_ref, wqkv_ref, wout_ref, wup_ref, wdown_ref,
        y_ref, gx_ref, gq_ref, go_ref, gu_ref, gd_ref, sv_ref,
        W, SP, CC, H2, CT, H2T, H1, H1T, GO, GOT, N1, R1, X1, N2, R2, DX1, DH1,
        COS, SIN, FH, FL, PHI, EE, VV, ATT, INV, AP, ST, TT, DA, ACT, DPRE, DQ,
        OS, OR, HS, HR, G, Q0, QX, QY, T2, Q2, U, ZR, AR, SV,
        local_sem, zs, zr, ags, agr, xs, xr, rs, rr, vs, vr,
    ) = refs
    rows = CC.shape[0] // 2
    dp = lax.axis_index("dp")
    z = lax.axis_index("mp")
    member = dp % GROUP
    c = member % 2
    bx = (member // 2) % 2
    by = member // 4
    nx = (dp + 2 - 4 * bx, z)
    ny = (dp + 4 - 8 * by, z)
    nc = (dp + 1 - 2 * c, z)
    nz = (None, (dp, z + 1 - 2 * (z % 2)), (dp, (z + 2) % 4), (dp, 3 - z))

    def place(yy, xx, cc):
        return pl.multiple_of((yy * 4 + xx * 2 + cc) * 96, 96)

    sends = []

    def send(src, dst, send_sem, recv_sem, device):
        copy = pltpu.make_async_remote_copy(
            src_ref=src, dst_ref=dst, send_sem=send_sem, recv_sem=recv_sem,
            device_id=device, device_id_type=MESH,
        )
        copy.start()
        sends.append(copy)

    def arrive(dst, recv_sem):
        pltpu.make_async_remote_copy(
            src_ref=dst, dst_ref=dst, send_sem=recv_sem, recv_sem=recv_sem,
            device_id=nc, device_id_type=MESH,
        ).wait_recv()

    barrier = pltpu.get_barrier_semaphore()
    for device in (nx, ny, nc, nz[1], nz[2], nz[3]):
        pl.semaphore_signal(barrier, inc=1, device_id=device, device_id_type=MESH)

    up_copy = pltpu.make_async_copy(wup_ref, W.at[4], local_sem.at[0])
    up_copy.start()
    down_copy = pltpu.make_async_copy(wdown_ref, W.at[5], local_sem.at[1])
    down_copy.start()

    qkv_own = wqkv_ref[...]
    packed = [qkv_own[:, h * 192 + s * 64:h * 192 + s * 64 + 64] for s in range(3) for h in range(3)]
    W[0] = jnp.concatenate(packed + [wout_ref[...].T], axis=1)
    feat = jnp.concatenate([feat_ref[h] for h in range(3)] + [jnp.zeros((64, 32), F32)], axis=1)
    SP[0, 0:64, :] = feat
    qkv_bias = vec_ref[7:8, 0:576]
    qkv_bias = jnp.concatenate(
        [qkv_bias[:, h * 192 + s * 64:h * 192 + s * 64 + 64] for s in range(3) for h in range(3)]
        + [jnp.zeros((1, 64), F32)], axis=1)
    for i in range(5):
        SP[0, 64 + i:65 + i, :] = qkv_bias[:, i * 128:i * 128 + 128]
    for i in range(6):
        SP[0, 72 + i:73 + i, :] = vec_ref[6:7, i * 128:i * 128 + 128]
    CC[0:rows, :] = jnp.concatenate([c_ref[...].astype(F32), jnp.zeros((rows - live, 768), F32)], axis=0).astype(BF16)

    pl.semaphore_wait(barrier, 6)

    own = pl.ds(place(by, bx, c), 96)
    for r in (1, 2, 3):
        send(SP.at[0], SP.at[r], zs.at[8 + r], zr.at[8 + r], nz[r])
        send(W.at[0, own], W.at[r, own], zs.at[r], agr.at[r, 0], nz[r])
    send(wup_ref.at[own], W.at[6, own], zs.at[6], agr.at[6, 0], nz[2])
    send(CC.at[0:rows], CC.at[rows:2 * rows], xs.at[0], xr.at[0], nz[1])
    send(wdown_ref.at[own], W.at[7, own], zs.at[7], agr.at[7, 0], nz[2])

    at_x = pl.ds(place(by, 1 - bx, c), 96)
    at_y = pl.ds(place(1 - by, bx, c), 96)
    at_d = pl.ds(place(1 - by, 1 - bx, c), 96)
    at_x0 = pl.ds(place(by, 1 - bx, c), 48)
    at_y1 = pl.ds(pl.multiple_of(place(1 - by, bx, c) + 48, 48), 48)
    at_d0 = pl.ds(place(1 - by, 1 - bx, c), 48)
    at_d1 = pl.ds(pl.multiple_of(place(1 - by, 1 - bx, c) + 48, 48), 48)

    def gather_a(b):
        arrive(W.at[b, own], agr.at[b, 0])
        send(W.at[b, own], W.at[b, own], ags.at[b, 0], agr.at[b, 1], nx)
        send(W.at[b, own], W.at[b, own], ags.at[b, 1], agr.at[b, 2], ny)
        send(W.at[b, own], W.at[b, own], ags.at[b, 2], agr.at[b, 5], nc)

    def gather_b(b):
        arrive(W.at[b, at_x], agr.at[b, 1])
        send(W.at[b, at_x0], W.at[b, at_x0], ags.at[b, 3], agr.at[b, 3], ny)
        send(W.at[b, at_x], W.at[b, at_x], ags.at[b, 4], agr.at[b, 6], nc)
        arrive(W.at[b, at_y], agr.at[b, 2])
        send(W.at[b, at_y1], W.at[b, at_y1], ags.at[b, 5], agr.at[b, 4], nx)
        send(W.at[b, at_y], W.at[b, at_y], ags.at[b, 6], agr.at[b, 7], nc)

    def gather_c(b):
        arrive(W.at[b, at_d0], agr.at[b, 3])
        arrive(W.at[b, at_d1], agr.at[b, 4])
        send(W.at[b, at_d], W.at[b, at_d], ags.at[b, 7], agr.at[b, 8], nc)

    def gather_d(b):
        for k, (yy, xx) in enumerate(((by, bx), (by, 1 - bx), (1 - by, bx), (1 - by, 1 - bx))):
            arrive(W.at[b, pl.ds(place(yy, xx, 1 - c), 96)], agr.at[b, 5 + k])

    rank = (0, 2, 0, 2, 0, 1, 2, 3)

    def reduce_1(g):
        send(G.at[g, :, 1 - c], Q0.at[g], rs.at[g, 0], rr.at[g, 0], nc)

    def reduce_2(g):
        arrive(Q0.at[g], rr.at[g, 0])
        for i in range(4):
            Q0[g, i] = (Q0[g, i].astype(F32) + G[g, i, c].astype(F32)).astype(BF16)
        for i in range(2):
            send(Q0.at[g, 2 * i + 1 - bx, 0:48], QX.at[g, i], rs.at[g, 1 + i], rr.at[g, 1 + i], nx)
            send(Q0.at[g, 2 * (1 - by) + i, 48:96], QY.at[g, i], rs.at[g, 3 + i], rr.at[g, 3 + i], ny)

    def reduce_3(g):
        for i in range(2):
            arrive(QX.at[g, i], rr.at[g, 1 + i])
            arrive(QY.at[g, i], rr.at[g, 3 + i])
        T2[g, 0] = (Q0[g, 2 * (1 - by) + bx, 0:48].astype(F32) + QX[g, 1 - by].astype(F32)).astype(BF16)
        T2[g, 1] = (Q0[g, 2 * by + 1 - bx, 48:96].astype(F32) + QY[g, 1 - bx].astype(F32)).astype(BF16)
        send(T2.at[g, 0], Q2.at[g, 0], rs.at[g, 5], rr.at[g, 5], ny)
        send(T2.at[g, 1], Q2.at[g, 1], rs.at[g, 6], rr.at[g, 6], nx)

    def reduce_4(g):
        arrive(Q2.at[g, 0], rr.at[g, 5])
        arrive(Q2.at[g, 1], rr.at[g, 6])
        mine = 2 * by + bx
        first = Q0[g, mine, 0:48].astype(F32) + QX[g, by].astype(F32) + Q2[g, 0].astype(F32)
        second = Q0[g, mine, 48:96].astype(F32) + QY[g, bx].astype(F32) + Q2[g, 1].astype(F32)
        total = jnp.concatenate([first, second], axis=0)
        if rank[g] == 0:
            return total
        U[g] = total.astype(BF16)
        send(U.at[g], ZR.at[g], rs.at[g, 7], rr.at[g, 7], nz[rank[g]])
        return None

    def landed(g):
        arrive(ZR.at[g], rr.at[g, 7])
        return ZR[g].astype(F32)

    ln1_gain, ln1_bias, b_out, ln2_gain, ln2_bias, b_down = (vec_ref[i:i + 1, :] for i in range(6))
    position = lax.broadcasted_iota(jnp.int32, (rows, 1), 0)
    key_mask = (position < len_ref[z]).astype(F32)
    trig = trig_ref[...]
    COS[...] = jnp.concatenate([trig[:, 0:64]] * 6, axis=1)
    SIN[...] = jnp.concatenate([trig[:, 64:128]] * 6, axis=1)
    row_q = lax.broadcasted_iota(jnp.int32, (192, 192), 0)
    col_q = lax.broadcasted_iota(jnp.int32, (192, 192), 1)
    head_mask = jnp.logical_and(row_q < 96, row_q // 32 == col_q // 64)
    row_f = lax.broadcasted_iota(jnp.int32, (384, 192), 0)
    col_f = lax.broadcasted_iota(jnp.int32, (384, 192), 1)
    feat_mask = row_f // 64 == col_f // 32

    X1[...] = jnp.concatenate([x_ref[...].astype(F32), jnp.zeros((rows - live, 768), F32)], axis=0)
    normed, factor = normalize(X1[...])
    N1[...] = normed
    R1[...] = factor
    first = (normed * ln1_gain + ln1_bias).astype(BF16)
    H1[...] = first
    AP[...] = jnp.zeros(AP.shape, BF16)

    def attend(r):
        bias = jnp.concatenate([SP[r, 64 + i:65 + i, :] for i in range(5)], axis=1)[:, 0:576]
        projected = dot_nn(H1[...], W[r, :, 0:576]) + bias
        both = projected[:, 0:384]
        value = projected[:, 384:576].astype(BF16)
        turned = both * COS[...] + swap_halves(both) * SIN[...]
        plain = SP[r, 0:64, :][:, 0:96]
        plain = jnp.concatenate([plain, plain], axis=1)
        block = jnp.where(feat_mask, jnp.concatenate([plain] * 6, axis=0), 0.0)
        f_high, f_low = split(block)
        FH[r] = f_high
        FL[r] = f_low
        t_high, t_low = split(turned)
        u = dot_nn(t_high, f_high) + dot_nn(t_high, f_low) + dot_nn(t_low, f_high)
        decay = jnp.exp(jnp.minimum(u, 0.0))
        EE[r] = decay
        phi32 = jnp.where(u > 0.0, u + 1.0, decay)
        phi = phi32.astype(BF16)
        PHI[r] = phi
        VV[r] = value
        masked = (phi.astype(F32) * key_mask).astype(BF16)
        pad = jnp.zeros((96, 192), F32)
        state = jnp.concatenate([dot_tn(masked, value)[96:192], pad], axis=0)
        total = jnp.concatenate([dot_tn(masked, jnp.ones((rows, 192), BF16))[96:192], pad], axis=0)
        state = jnp.where(head_mask, state, 0.0)
        total = jnp.where(head_mask, total, 0.0)
        ST[r] = state
        TT[r] = total
        s_high, s_low = split(state)
        k_high, k_low = split(total)
        numer = dot_nn(phi, s_high) + dot_nn(phi, s_low)
        inverse = 1.0 / (dot_nn(phi, k_high) + dot_nn(phi, k_low))
        attended = numer * inverse
        ATT[r] = attended
        INV[r] = inverse
        AP[r, :, 64:256] = attended.astype(BF16)
        X1[...] += dot_nt(AP[r], W[r, :, 512:768])

    gather_a(1)
    attend(0)
    gather_b(1)
    gather_a(2)
    gather_c(1)
    gather_b(2)
    gather_a(3)
    gather_d(1)
    arrive(SP.at[1], zr.at[9])
    attend(1)
    gather_c(2)
    gather_b(3)
    gather_a(6)
    gather_d(2)
    arrive(SP.at[2], zr.at[10])
    attend(2)
    gather_c(3)
    gather_b(6)
    gather_a(7)
    gather_d(3)
    arrive(SP.at[3], zr.at[11])
    attend(3)

    middle = X1[...] + b_out
    X1[...] = middle
    normed, factor = normalize(middle)
    N2[...] = normed
    R2[...] = factor
    second = (normed * ln2_gain + ln2_bias).astype(BF16)
    H2[0:rows, :] = second
    send(H2.at[0:rows], H2.at[rows:2 * rows], xs.at[1], xr.at[1], nz[1])

    gather_c(6)
    gather_b(7)
    gather_d(6)
    up_copy.wait()
    down_copy.wait()
    arrive(CC.at[rows:2 * rows], xr.at[0])
    up = (4, 6)
    down = (5, 7)
    DA[0] = dot_nt(CC[...], W[5])
    gather_c(7)

    def feed(q, s):
        part = pl.ds(s * rows, rows)
        bias = jnp.concatenate([SP[2 * q, 72 + i:73 + i, :] for i in range(6)], axis=1)
        pre = dot_nn(H2[part], W[up[q]]) + bias
        half = 0.5 * (1.0 + lax.erf(pre * (0.5 ** 0.5)))
        ACT[q, part] = (pre * half).astype(BF16)
        slope = half + pre * jnp.exp(-0.5 * pre * pre) * (0.5 / np.pi) ** 0.5
        DPRE[q, part] = (DA[q, part] * slope).astype(BF16)

    feed(0, 0)
    gather_d(7)
    DA[1] = dot_nt(CC[...], W[7])
    feed(1, 0)
    CT[...] = CC[...].T
    H1T[...] = H1[...].T
    arrive(H2.at[rows:2 * rows], xr.at[1])
    feed(0, 1)
    feed(1, 1)
    theirs = pl.ds(rows, rows)
    mine = pl.ds(0, rows)
    HS[...] = (dot_nt(DPRE[0, theirs], W[4]) + dot_nt(DPRE[1, theirs], W[6])).astype(BF16)
    send(HS, HR, xs.at[2], xr.at[2], nz[1])

    def store_block(g, left, right):
        for n in range(3):
            cols = slice(n * 256, n * 256 + 256)
            G[g, :, :, :, cols] = dot_nn(left, right[:, cols]).astype(BF16).reshape(4, 2, 96, 256)

    store_block(0, CT[...], ACT[0])
    reduce_1(0)
    store_block(1, CT[...], ACT[1])
    reduce_1(1)
    reduce_2(0)
    H2T[...] = H2[...].T
    store_block(2, H2T[...], DPRE[0])
    reduce_1(2)
    reduce_2(1)
    store_block(3, H2T[...], DPRE[1])
    reduce_1(3)
    reduce_2(2)
    OS[...] = (dot_nn(ACT[0, theirs], W[5]) + dot_nn(ACT[1, theirs], W[7])).astype(BF16)
    SV[...] = jnp.zeros(SV.shape, F32)
    for q in range(2):
        SV[10 + q:11 + q, :] = column_sum(DPRE[q].astype(F32))
    own_back = dot_nt(DPRE[0, mine], W[4]) + dot_nt(DPRE[1, mine], W[6])
    reduce_2(3)

    arrive(HR, xr.at[2])
    send(OS, OR, xs.at[3], xr.at[3], nz[1])
    own_back = own_back + HR[...].astype(F32)
    cot = CC[mine].astype(F32)
    SV[3:4, :] = column_sum(own_back * N2[...])
    SV[4:5, :] = column_sum(own_back)
    SV[5:6, :] = column_sum(cot)
    dx1 = cot + norm_back(own_back, ln2_gain, N2[...], R2[...])
    DX1[...] = dx1
    branch = dx1.astype(BF16)
    GO[...] = branch
    SV[2:3, :] = column_sum(branch.astype(F32))
    reduce_3(0)
    GOT[...] = GO[...].T
    DH1[...] = jnp.zeros(DH1.shape, F32)

    def attend_back(r):
        da = dot_nn(GO[...], W[r, :, 512:768])[:, 64:256]
        phi = PHI[r]
        dnum = da * INV[r]
        drest = -(dnum * ATT[r])
        n_high, n_low = split(dnum)
        d_high, d_low = split(drest)
        s_high, s_low = split(ST[r])
        k_high, k_low = split(TT[r])
        dphi = dot_nt(n_high, s_high) + dot_nt(n_high, s_low) + dot_nt(n_low, s_high)
        dphi += dot_nt(d_high, k_high) + dot_nt(d_high, k_low) + dot_nt(d_low, k_high)
        pad = jnp.zeros((96, 192), F32)
        dstate = jnp.where(head_mask, dot_tn(phi, n_high) + dot_tn(phi, n_low), 0.0)
        dtotal = jnp.where(head_mask, dot_tn(phi, d_high) + dot_tn(phi, d_low), 0.0)
        a_high, a_low = split(jnp.concatenate([pad, dstate[0:96]], axis=0))
        b_high, b_low = split(jnp.concatenate([pad, dtotal[0:96]], axis=0))
        ones = jnp.ones((16, 192), BF16)
        dkey = dot_nt(VV[r], a_high) + dot_nt(VV[r], a_low)
        dkey += (dot_nt(ones, b_high) + dot_nt(ones, b_low))[0:1, :]
        dphi += key_mask * dkey
        dvalue = key_mask * (dot_nn(phi, a_high) + dot_nn(phi, a_low))
        u_high, u_low = split(dphi * EE[r])
        back = dot_nt(u_high, FH[r]) + dot_nt(u_high, FL[r]) + dot_nt(u_low, FH[r])
        back = back * COS[...] - swap_halves(back) * SIN[...]
        DQ[:, 0:384] = back.astype(BF16)
        DQ[:, 384:576] = dvalue.astype(BF16)
        SV[6 + r:7 + r, 0:576] = column_sum(DQ[...].astype(F32))
        DH1[...] += dot_nt(DQ[...], W[r, :, 0:576])

    def store_attention(r):
        g = 4 + r
        for n in range(2):
            cols = slice(n * 256, n * 256 + 256)
            G[g, :, :, :, cols] = dot_nn(H1T[...], DQ[:, cols]).astype(BF16).reshape(4, 2, 96, 256)
        edge = jnp.concatenate(
            [dot_nn(H1T[...], DQ[:, 512:576]), dot_nn(GOT[...], AP[r, :, 64:256])], axis=1)
        G[g, :, :, :, 512:768] = edge.astype(BF16).reshape(4, 2, 96, 256)

    attend_back(3)
    store_attention(3)
    reduce_1(7)
    reduce_3(1)
    down_own = reduce_4(0)
    attend_back(2)
    store_attention(2)
    reduce_1(6)
    reduce_2(7)
    reduce_3(2)
    reduce_4(1)
    attend_back(1)
    store_attention(1)
    reduce_1(5)
    reduce_2(6)
    reduce_3(3)
    up_own = reduce_4(2)
    attend_back(0)
    store_attention(0)
    reduce_1(4)
    reduce_2(5)
    reduce_4(3)
    reduce_3(7)

    first_back = DH1[...]
    SV[0:1, :] = column_sum(first_back * N1[...])
    SV[1:2, :] = column_sum(first_back)
    send(SV, AR.at[0], vs.at[0], vr.at[0], nc)
    gx_ref[...] = (DX1[...] + norm_back(first_back, ln1_gain, N1[...], R1[...]))[0:live]
    reduce_2(4)
    arrive(AR.at[0], vr.at[0])
    AR[1] = SV[...] + AR[0]
    send(AR.at[1], AR.at[2], vs.at[1], vr.at[1], nx)
    reduce_4(7)
    reduce_3(6)
    gd_ref[...] = down_own + landed(1)
    gu_ref[...] = up_own + landed(3)

    output = dot_nn(ACT[0, mine], W[5]) + dot_nn(ACT[1, mine], W[7])
    arrive(OR, xr.at[3])
    output = X1[...] + output + OR[...].astype(F32) + b_down
    y_ref[...] = output[0:live].astype(BF16)

    arrive(AR.at[2], vr.at[1])
    AR[3] = AR[1] + AR[2]
    send(AR.at[3], AR.at[4], vs.at[2], vr.at[2], ny)
    reduce_3(5)
    reduce_4(6)
    arrive(AR.at[4], vr.at[2])
    AR[5] = AR[3] + AR[4]
    for r in (1, 2, 3):
        send(AR.at[5], AR.at[5 + r], vs.at[2 + r], vr.at[2 + r], nz[r])
    reduce_3(4)
    reduce_4(5)
    block = reduce_4(4)
    for r in (1, 2, 3):
        arrive(AR.at[5 + r], vr.at[2 + r])
    sv_ref[0:6, :] = AR[5, 0:6, :] + AR[6, 0:6, :] + AR[7, 0:6, :] + AR[8, 0:6, :]
    sv_ref[6:7, :] = AR[5, 10:11, :] + AR[7, 11:12, :]
    bias = AR[5, 6:7, :] + AR[6, 7:8, :] + AR[7, 8:9, :] + AR[8, 9:10, :]
    bias = [bias[:, s * 192 + h * 64:s * 192 + h * 64 + 64] for h in range(3) for s in range(3)]
    sv_ref[7:8, :] = jnp.concatenate(bias + [jnp.zeros((1, 192), F32)], axis=1)
    for r in (1, 2, 3):
        block = block + landed(4 + r)
    gq_ref[...] = jnp.concatenate(
        [block[:, s * 192 + h * 64:s * 192 + h * 64 + 64] for h in range(3) for s in range(3)], axis=1)
    go_ref[...] = block[:, 576:768]
    for copy in sends:
        copy.wait_send()


def trig_table(live, rows, head_dim):
    half = head_dim // 2
    freq = (10000.0 ** (-np.arange(half, dtype=np.float32) * 2.0 / head_dim)).astype(np.float32)
    angle = (np.arange(rows, dtype=np.float32)[:, None] * freq[None, :]).astype(np.float64)
    cosine, sine = np.cos(angle), np.sin(angle)
    table = np.concatenate([cosine, cosine, -sine, sine], axis=1) * head_dim ** (-0.25)
    return table.astype(np.float32)


def local(
    n_dp, layer_input, lengths, ln1_gain, ln1_bias, w_qkv, b_qkv, features, w_out, b_out,
    ln2_gain, ln2_bias, w_up, b_up, w_down, b_down, cotangent,
):
    live, width = layer_input.shape
    rows = -(-live // 16) * 16
    vectors = jnp.stack([
        ln1_gain, ln1_bias, b_out, ln2_gain, ln2_bias, b_down, b_up,
        jnp.pad(b_qkv, (0, width - b_qkv.shape[0])),
    ])
    trig = jnp.asarray(trig_table(live, rows, features.shape[1]))
    vmem = pl.BlockSpec(memory_space=pltpu.VMEM)
    smem = pl.BlockSpec(memory_space=pltpu.SMEM)
    anywhere = pl.BlockSpec(memory_space=pl.ANY)
    dma = pltpu.SemaphoreType.DMA

    def buf(*shape):
        return pltpu.VMEM(shape, BF16)

    def wide(*shape):
        return pltpu.VMEM(shape, F32)

    outs = pl.pallas_call(
        functools.partial(layer_kernel, live),
        out_shape=[
            jax.ShapeDtypeStruct((live, width), BF16),
            jax.ShapeDtypeStruct((live, width), F32),
            jax.ShapeDtypeStruct((96, 576), F32),
            jax.ShapeDtypeStruct((96, 192), F32),
            jax.ShapeDtypeStruct((96, 768), F32),
            jax.ShapeDtypeStruct((96, 768), F32),
            jax.ShapeDtypeStruct((8, 768), F32),
        ],
        in_specs=[vmem, vmem, smem] + [vmem] * 5 + [anywhere] * 2,
        out_specs=[vmem] * 7,
        scratch_shapes=[
            buf(8, 768, 768), wide(4, 80, 128), buf(2 * rows, 768), buf(2 * rows, 768),
            buf(768, 2 * rows), buf(768, 2 * rows), buf(rows, 768), buf(768, rows),
            buf(rows, 768), buf(768, rows), wide(rows, 768), wide(rows, 1), wide(rows, 768),
            wide(rows, 768), wide(rows, 1), wide(rows, 768), wide(rows, 768),
            wide(rows, 384), wide(rows, 384), buf(4, 384, 192), buf(4, 384, 192),
            buf(4, rows, 192), wide(4, rows, 192), buf(4, rows, 192), wide(4, rows, 192),
            wide(4, rows, 192), buf(4, rows, 256), wide(4, 192, 192), wide(4, 192, 192),
            wide(2, 2 * rows, 768), buf(2, 2 * rows, 768), buf(2, 2 * rows, 768), buf(rows, 576),
            buf(rows, 768), buf(rows, 768), buf(rows, 768), buf(rows, 768),
            buf(8, 4, 2, 96, 768), buf(8, 4, 96, 768), buf(8, 2, 48, 768), buf(8, 2, 48, 768),
            buf(8, 2, 48, 768), buf(8, 2, 48, 768), buf(8, 96, 768), buf(8, 96, 768),
            wide(9, 16, 768), wide(16, 768),
            dma((2,)), dma((12,)), dma((12,)), dma((8, 8)), dma((8, 9)), dma((4,)), dma((4,)),
            dma((8, 8)), dma((8, 8)), dma((6,)), dma((6,)),
        ],
        compiler_params=pltpu.CompilerParams(
            collective_id=0, has_side_effects=True, vmem_limit_bytes=67043328),
    )(layer_input, cotangent, lengths, vectors, features, trig, w_qkv, w_out, w_up, w_down)
    output, grad_x, qkv_piece, out_piece, up_piece, down_piece, small = outs
    common, up_bias, qkv_bias = small[0:6], small[6], small[7, 0:576]
    out_piece, down_piece = out_piece.T, down_piece.T
    if n_dp != GROUP:
        member = lax.axis_index("dp") % GROUP

        def spread(piece, axis):
            shape = list(piece.shape)
            shape[axis] = shape[axis] * GROUP
            start = [0, 0]
            start[axis] = member * piece.shape[axis]
            whole = lax.dynamic_update_slice(jnp.zeros(shape, F32), piece, start)
            return lax.psum_scatter(whole, "dp", scatter_dimension=axis, tiled=True)

        qkv_piece, out_piece = spread(qkv_piece, 0), spread(out_piece, 1)
        up_piece, down_piece = spread(up_piece, 0), spread(down_piece, 1)
        common, up_bias, qkv_bias = jax.tree.map(
            lambda part: lax.psum(part, "dp") / GROUP, (common, up_bias, qkv_bias))
    return (
        output, grad_x, common[0], common[1], qkv_piece, qkv_bias, out_piece, common[2],
        common[3], common[4], up_piece, up_bias, down_piece, common[5],
    )


def solution(mesh):
    rows, cols = P(("dp", "mp"), None), P(None, "mp")
    placed = (
        rows, P("dp"), P(), P(), cols, P("mp"), P("mp", None, None), P("mp", None), P(),
        P(), P(), cols, P("mp"), P("mp", None), P(), rows,
    )
    return jax.shard_map(
        functools.partial(local, mesh.shape["dp"]),
        mesh=mesh,
        in_specs=placed,
        out_specs=(
            rows, rows, P(), P(), P("dp", "mp"), P("mp"), P("mp", "dp"), P(),
            P(), P(), P("dp", "mp"), P("mp"), P("mp", "dp"), P(),
        ),
        check_vma=False,
    )
```

time: 411 us -> 138 us (0.34)
  blocking collectives: 161 us -> 0 us
  Pallas kernels: 0 us -> 117 us
  waiting for transfers between devices: 112 us -> 0 us
  matrix products: 54.1 us -> 0 us
  other arithmetic: 22.2 us -> 0 us
  local copies, waits for them, and re-layouts: 35.5 us -> 19.4 us
  between operations: 15.7 us -> 0.68 us
  starting transfers between devices: 8.88 us -> 0 us
    pallas_call x0 -> x1, Pallas kernels: none -> 117 us  [local(): pl.pallas_call(functools.partial(layer_kernel, live), out_shape=[jax.Shap...]
    unnamed x3 -> x0, blocking collectives: 109 us -> none
    all_gather x4 -> x0, waiting for transfers between devices: 93.9 us -> none  [the longest x1 31.9 us: local(): branch_rows = lax.all_gather(grad_branch, 'mp', axis=0, tiled=True)]
    psum x2 -> x0, blocking collectives: 51.6 us -> none  [the longest x1 38.1 us: local(): lax.psum((grad_ln1_gain, grad_ln1_bias, grad_b_out, grad_ln2_gain, grad_l...]
    dot_general x23 -> x0, matrix products: 51.5 us -> none  [the longest x4 15.5 us: contract_last(): lax.dot_general(left, right, (((1,), (1,)), ((), ())), preferred_element_...]
    reduce_scatter x3 -> x0, waiting for transfers between devices: 15.2 us -> none  [the longest x1 15.2 us: local(): lax.psum_scatter(grad_w_qkv, 'dp', scatter_dimension=0, tiled=True)]
    unnamed x111 -> x16, local copies, waits for them, and re-layouts: 20.4 us -> 10.1 us
    reduce_sum x10 -> x0, other arithmetic: 8.46 us -> none  [the longest x1 2.12 us: local(): grad_b_out = jnp.sum(grad_branch.astype(jnp.float32), axis=0)]
  transfers between devices with their start and end apart: 12 -> 0, of which waited for: 6 -> 0; matrix products, arithmetic and copies ran while one was open for 39% -> 0% of each run, Pallas kernels for 0% -> 0%
where the time goes in v1:
time: 138 us; the launch traced here: 137 us
  Pallas kernels  117 us (85%)
  local copies, waits for them, and re-layouts  19.4 us (14%)
    pallas_call x1, Pallas kernels, local(): pl.pallas_call(functools.partial(layer_kernel, live), out_shape=[jax.Shap...  117 us
    unnamed x16, local copies, waits for them, and re-layouts  10.1 us
    another operation x9, local copies, waits for them, and re-layouts, local(): jnp.stack([ln1_gain, ln1_bias, b_out, ln2_gain, ln2_bias, b_down, b_up, j...  5.48 us

profile of v1, /device:TPU:0, one launch (start us, length us, event | category | flops | bytes accessed | tf_op | source)
XLA Modules:
  0.0 136.9 jit_solution(10848420183062618462)
XLA Ops:
  0.6 0.7 stack.27
  1.3 0.7 stack.28
  2.0 0.7 stack.29
  2.7 0.7 stack.30
  3.4 0.7 stack.31
  4.1 0.7 stack.33
  4.8 0.7 stack.32
  5.5 0.7 pad.4
  6.2 0.6 stack.35.refs_3_
  6.8 1.5 %copy.31.refs_4_ = f32[3,64,32]{2,1,0:T(8,128)} copy(f32[3,64,32]{1,2,0:T(8,128)} %param.23) | data formatting | bytes 49152 | tf_op args[6]
  8.4 2.2 %copy.32.refs_6_ = bf16[768,576]{1,0:T(8,128)(2,1)} copy(bf16[768,576]{0,1:T(8,128)(2,1)} %param.21) | data formatting | bytes 1769472 | tf_op args[4]
  10.6 116.9 %shard_map.272 = (bf16[202,768]{1,0:T(8,128)(2,1)}, f32[202,768]{1,0:T(8,128)}, f32[96,576]{1,0:T(8,128)}, f32[96,192]{1,0:T(8,128)}, f32[96,768]{1,0:T(8,128)}, /*index=5*/f32[96,768]{1,0:T(8,128)}, f32[8,768]{1,0:T(8,128)}) custom-call(bf16[202,768]{1,0:T(8,128)(2,1)} %refs_0_.1, bf16[202,768]{1,0:T(8,128)(2,1)} %refs_1_.1, s32[4]{0:T(128)} %refs_2_.1, ...), custom_call_target="tpu_custom_call" | custom-call | tf_op jit(solution)/shard_map/pallas_call | solution.py:509
  127.5 0.0 copy-start
  127.5 0.0 copy-start.3
  127.5 1.4 %slice_reduce_fusion.7 = f32[576]{0:T(1024)} fusion(f32[8,768]{1,0:T(8,128)} %get-tuple-element.23), kind=kLoop, calls=%fused_computation.7 | loop fusion | bytes 4608 | tf_op jit(solution)/shard_map/slice | solution.py:542
  128.9 1.7 %slice_reduce_fusion = (f32[768]{0:T(1024)}, f32[768]{0:T(1024)}, f32[768]{0:T(1024)}, f32[768]{0:T(1024)}, f32[768]{0:T(1024)}, /*index=5*/f32[768]{0:T(1024)}, f32[768]{0:T(1024)}) fusion(f32[8,768]{1,0:T(8,128)} %get-tuple-element.23), kind=kLoop, calls=%fused_computation | loop fusion | bytes 43008 | tf_op jit(solution)/shard_map/slice | solution.py:561
  130.6 1.6 %copy.33 = f32[192,96]{1,0:T(8,128)} copy(f32[192,96]{0,1:T(8,128)} %bitcast.3) | data formatting | bytes 147456
  132.2 0.0 copy-start.2
  132.2 1.8 %copy.39 = bf16[202,768]{1,0:T(8,128)(2,1)} copy(bf16[202,768]{1,0:T(8,128)(2,1)} %get-tuple-element.63) | data formatting | bytes 620544
  134.0 0.0 copy-done
  134.0 0.0 copy-start.1
  134.0 0.8 copy.40
  134.8 0.0 copy-done.3
  134.8 0.7 copy.41
  135.5 0.0 copy-done.2
  135.5 0.7 copy.42
  136.2 0.0 copy-done.1
  136.2 0.7 copy.43
  (1 shorter events, 0.0 us)
Async XLA Ops:
  127.5 6.5 %copy-start = (f32[202,768]{1,0:T(8,128)S(1)}, f32[202,768]{1,0:T(8,128)}, u32[]{:S(2)}) copy-start(f32[202,768]{1,0:T(8,128)} %get-tuple-element.64) | copy-start | bytes 1861636
  127.5 7.3 %copy-start.3 = (f32[96,576]{1,0:T(8,128)S(1)}, f32[96,576]{1,0:T(8,128)}, u32[]{:S(2)}) copy-start(f32[96,576]{1,0:T(8,128)} %get-tuple-element.67) | copy-start | bytes 663556
  132.2 3.3 %copy-start.2 = (f32[96,768]{1,0:T(8,128)S(1)}, f32[96,768]{1,0:T(8,128)}, u32[]{:S(2)}) copy-start(f32[96,768]{1,0:T(8,128)} %get-tuple-element.73) | copy-start | bytes 884740
  134.0 2.2 %copy-start.1 = (f32[96,768]{1,0:T(8,128)S(1)}, f32[96,768]{1,0:T(8,128)}, u32[]{:S(2)}) copy-start(f32[96,768]{1,0:T(8,128)} %get-tuple-element.27) | copy-start | bytes 884740

commit v2 on v1

--- a/solution.py
+++ b/solution.py
@@ -59,11 +59,12 @@
 
 def layer_kernel(live, *refs):
     (
-        x_ref, c_ref, len_ref, vec_ref, feat_ref, trig_ref, wqkv_ref, wout_ref, wup_ref, wdown_ref,
+        x_ref, c_ref, len_ref, ln1_gain_ref, ln1_bias_ref, b_out_ref, ln2_gain_ref, ln2_bias_ref,
+        b_down_ref, b_up_ref, b_qkv_ref, feat_ref, trig_ref, wqkv_ref, wout_ref, wup_ref, wdown_ref,
         y_ref, gx_ref, gq_ref, go_ref, gu_ref, gd_ref, sv_ref,
         W, SP, CC, H2, CT, H2T, H1, H1T, GO, GOT, N1, R1, X1, N2, R2, DX1, DH1,
-        COS, SIN, FH, FL, PHI, EE, VV, ATT, INV, AP, ST, TT, DA, ACT, DPRE, DQ,
-        OS, OR, HS, HR, G, Q0, QX, QY, T2, Q2, U, ZR, AR, SV,
+        COS, SIN, FH, FL, PHI, EE, VV, ATT, INV, AB, ST, TT, DA, ACT, DPRE, DQ,
+        OS, OR, HS, HR, G, Q0, QX, QY, T2, Q2, U, ZR, EV, LV,
         local_sem, zs, zr, ags, agr, xs, xr, rs, rr, vs, vr,
     ) = refs
     rows = CC.shape[0] // 2
@@ -101,35 +102,61 @@
     for device in (nx, ny, nc, nz[1], nz[2], nz[3]):
         pl.semaphore_signal(barrier, inc=1, device_id=device, device_id_type=MESH)
 
-    up_copy = pltpu.make_async_copy(wup_ref, W.at[4], local_sem.at[0])
-    up_copy.start()
-    down_copy = pltpu.make_async_copy(wdown_ref, W.at[5], local_sem.at[1])
-    down_copy.start()
-
-    qkv_own = wqkv_ref[...]
-    packed = [qkv_own[:, h * 192 + s * 64:h * 192 + s * 64 + 64] for s in range(3) for h in range(3)]
-    W[0] = jnp.concatenate(packed + [wout_ref[...].T], axis=1)
-    feat = jnp.concatenate([feat_ref[h] for h in range(3)] + [jnp.zeros((64, 32), F32)], axis=1)
-    SP[0, 0:64, :] = feat
-    qkv_bias = vec_ref[7:8, 0:576]
+    loads = [
+        pltpu.make_async_copy(source, target, local_sem.at[i])
+        for i, (source, target) in enumerate((
+            (wqkv_ref, W.at[0, 0:576]), (wout_ref, W.at[0, 576:768]),
+            (wup_ref, W.at[4]), (wdown_ref, W.at[5])))
+    ]
+    for load in loads:
+        load.start()
+
+    SP[0, 0:64, 0:96] = feat_ref[...].reshape(96, 64).T
+    qkv_bias = b_qkv_ref[...].reshape(1, 576)
     qkv_bias = jnp.concatenate(
         [qkv_bias[:, h * 192 + s * 64:h * 192 + s * 64 + 64] for s in range(3) for h in range(3)]
         + [jnp.zeros((1, 64), F32)], axis=1)
     for i in range(5):
         SP[0, 64 + i:65 + i, :] = qkv_bias[:, i * 128:i * 128 + 128]
+    up_bias = b_up_ref[...].reshape(1, 768)
     for i in range(6):
-        SP[0, 72 + i:73 + i, :] = vec_ref[6:7, i * 128:i * 128 + 128]
+        SP[0, 72 + i:73 + i, :] = up_bias[:, i * 128:i * 128 + 128]
     CC[0:rows, :] = jnp.concatenate([c_ref[...].astype(F32), jnp.zeros((rows - live, 768), F32)], axis=0).astype(BF16)
 
     pl.semaphore_wait(barrier, 6)
 
     own = pl.ds(place(by, bx, c), 96)
+    inner = jnp.logical_or(z == 1, z == 2)
+    second_rank = jnp.where(inner, 3, 2)
+    third_rank = jnp.where(inner, 2, 3)
+
+    def send_if(condition, src, dst, send_sem, recv_sem, device):
+        copy = pltpu.make_async_remote_copy(
+            src_ref=src, dst_ref=dst, send_sem=send_sem, recv_sem=recv_sem,
+            device_id=device, device_id_type=MESH,
+        )
+
+        @pl.when(condition)
+        def _():
+            copy.start()
+
+        late_sends.append((condition, copy))
+
+    late_sends = []
+    in_qkv = member < 6
+    out_rows = pl.ds(pl.multiple_of(jnp.maximum(own.start - 576, 0), 96), 96)
+    qkv_rows = pl.ds(pl.multiple_of(jnp.minimum(own.start, 480), 96), 96)
+    for r, condition in ((1, None), (3, inner)):
+        for part, source in ((in_qkv, wqkv_ref.at[qkv_rows]), (jnp.logical_not(in_qkv), wout_ref.at[out_rows])):
+            both = part if condition is None else jnp.logical_and(part, condition)
+            send_if(both, source, W.at[r, own], zs.at[r], agr.at[r, 0], nz[r])
+    half = pl.ds(pl.multiple_of(c * 40, 8), 40)
+    other_half = pl.ds(pl.multiple_of((1 - c) * 40, 8), 40)
     for r in (1, 2, 3):
-        send(SP.at[0], SP.at[r], zs.at[8 + r], zr.at[8 + r], nz[r])
-        send(W.at[0, own], W.at[r, own], zs.at[r], agr.at[r, 0], nz[r])
-    send(wup_ref.at[own], W.at[6, own], zs.at[6], agr.at[6, 0], nz[2])
-    send(CC.at[0:rows], CC.at[rows:2 * rows], xs.at[0], xr.at[0], nz[1])
-    send(wdown_ref.at[own], W.at[7, own], zs.at[7], agr.at[7, 0], nz[2])
+        send(SP.at[0, half], SP.at[r, half], zs.at[8 + r], zr.at[r], nz[r])
+
+    def forward(b, to_rank, slot):
+        send_if(inner, W.at[b, own], W.at[slot, own], zs.at[3 + slot + to_rank], agr.at[slot, 0], nz[to_rank])
 
     at_x = pl.ds(place(by, 1 - bx, c), 96)
     at_y = pl.ds(place(1 - by, bx, c), 96)
@@ -157,6 +184,17 @@
         arrive(W.at[b, at_d0], agr.at[b, 3])
         arrive(W.at[b, at_d1], agr.at[b, 4])
         send(W.at[b, at_d], W.at[b, at_d], ags.at[b, 7], agr.at[b, 8], nc)
+
+    def gather_small(r):
+        arrive(SP.at[r, half], zr.at[r])
+        send(SP.at[r, half], SP.at[r, half], zs.at[12 + r], zr.at[4 + r], nc)
+
+    def small_done(r):
+        arrive(SP.at[r, other_half], zr.at[4 + r])
+
+    def qkv_rows_of(r):
+        return jnp.concatenate(
+            [W[r, h * 192 + s * 64:h * 192 + s * 64 + 64, :] for s in range(3) for h in range(3)], axis=0)
 
     def gather_d(b):
         for k, (yy, xx) in enumerate(((by, bx), (by, 1 - bx), (1 - by, bx), (1 - by, 1 - bx))):
@@ -201,7 +239,9 @@
         arrive(ZR.at[g], rr.at[g, 7])
         return ZR[g].astype(F32)
 
-    ln1_gain, ln1_bias, b_out, ln2_gain, ln2_bias, b_down = (vec_ref[i:i + 1, :] for i in range(6))
+    ln1_gain, ln1_bias, b_out, ln2_gain, ln2_bias, b_down = (
+        ref[...].reshape(1, 768)
+        for ref in (ln1_gain_ref, ln1_bias_ref, b_out_ref, ln2_gain_ref, ln2_bias_ref, b_down_ref))
     position = lax.broadcasted_iota(jnp.int32, (rows, 1), 0)
     key_mask = (position < len_ref[z]).astype(F32)
     trig = trig_ref[...]
@@ -220,11 +260,10 @@
     R1[...] = factor
     first = (normed * ln1_gain + ln1_bias).astype(BF16)
     H1[...] = first
-    AP[...] = jnp.zeros(AP.shape, BF16)
 
     def attend(r):
         bias = jnp.concatenate([SP[r, 64 + i:65 + i, :] for i in range(5)], axis=1)[:, 0:576]
-        projected = dot_nn(H1[...], W[r, :, 0:576]) + bias
+        projected = dot_nt(H1[...], qkv_rows_of(r)) + bias
         both = projected[:, 0:384]
         value = projected[:, 384:576].astype(BF16)
         turned = both * COS[...] + swap_halves(both) * SIN[...]
@@ -257,31 +296,40 @@
         attended = numer * inverse
         ATT[r] = attended
         INV[r] = inverse
-        AP[r, :, 64:256] = attended.astype(BF16)
-        X1[...] += dot_nt(AP[r], W[r, :, 512:768])
+        mixed = attended.astype(BF16)
+        AB[r] = mixed
+        X1[...] += dot_nn(mixed, W[r, 576:768, :])
 
     gather_a(1)
+    forward(1, 3, 2)
+    for load in loads:
+        load.wait()
     attend(0)
+    gather_a(second_rank)
+    forward(3, 1, 2)
+    send(wup_ref.at[own], W.at[6, own], zs.at[2], agr.at[6, 0], nz[2])
+    for r in (1, 2, 3):
+        gather_small(r)
     gather_b(1)
-    gather_a(2)
     gather_c(1)
-    gather_b(2)
-    gather_a(3)
+    gather_a(third_rank)
+    forward(2, 1, 3)
+    send(wdown_ref.at[own], W.at[7, own], zs.at[0], agr.at[7, 0], nz[2])
+    send(CC.at[0:rows], CC.at[rows:2 * rows], xs.at[0], xr.at[0], nz[1])
+    for r in (1, 2, 3):
+        small_done(r)
     gather_d(1)
-    arrive(SP.at[1], zr.at[9])
     attend(1)
-    gather_c(2)
-    gather_b(3)
+    gather_b(second_rank)
+    gather_c(second_rank)
     gather_a(6)
-    gather_d(2)
-    arrive(SP.at[2], zr.at[10])
-    attend(2)
-    gather_c(3)
-    gather_b(6)
+    gather_d(second_rank)
+    attend(second_rank)
+    gather_b(third_rank)
     gather_a(7)
-    gather_d(3)
-    arrive(SP.at[3], zr.at[11])
-    attend(3)
+    gather_c(third_rank)
+    gather_d(third_rank)
+    attend(third_rank)
 
     middle = X1[...] + b_out
     X1[...] = middle
@@ -292,11 +340,10 @@
     H2[0:rows, :] = second
     send(H2.at[0:rows], H2.at[rows:2 * rows], xs.at[1], xr.at[1], nz[1])
 
+    gather_b(6)
     gather_c(6)
     gather_b(7)
     gather_d(6)
-    up_copy.wait()
-    down_copy.wait()
     arrive(CC.at[rows:2 * rows], xr.at[0])
     up = (4, 6)
     down = (5, 7)
@@ -319,20 +366,21 @@
     CT[...] = CC[...].T
     H1T[...] = H1[...].T
     arrive(H2.at[rows:2 * rows], xr.at[1])
-    feed(0, 1)
-    feed(1, 1)
     theirs = pl.ds(rows, rows)
     mine = pl.ds(0, rows)
-    HS[...] = (dot_nt(DPRE[0, theirs], W[4]) + dot_nt(DPRE[1, theirs], W[6])).astype(BF16)
-    send(HS, HR, xs.at[2], xr.at[2], nz[1])
 
     def store_block(g, left, right):
         for n in range(3):
             cols = slice(n * 256, n * 256 + 256)
             G[g, :, :, :, cols] = dot_nn(left, right[:, cols]).astype(BF16).reshape(4, 2, 96, 256)
 
+    feed(0, 1)
     store_block(0, CT[...], ACT[0])
     reduce_1(0)
+    feed(1, 1)
+    HS[...] = (dot_nt(DPRE[0, theirs], W[4]) + dot_nt(DPRE[1, theirs], W[6])).astype(BF16)
+    send(HS, HR, xs.at[2], xr.at[2], nz[1])
+
     store_block(1, CT[...], ACT[1])
     reduce_1(1)
     reduce_2(0)
@@ -344,9 +392,8 @@
     reduce_1(3)
     reduce_2(2)
     OS[...] = (dot_nn(ACT[0, theirs], W[5]) + dot_nn(ACT[1, theirs], W[7])).astype(BF16)
-    SV[...] = jnp.zeros(SV.shape, F32)
     for q in range(2):
-        SV[10 + q:11 + q, :] = column_sum(DPRE[q].astype(F32))
+        EV[0, 4 + q:5 + q, :] = column_sum(DPRE[q].astype(F32))
     own_back = dot_nt(DPRE[0, mine], W[4]) + dot_nt(DPRE[1, mine], W[6])
     reduce_2(3)
 
@@ -354,20 +401,20 @@
     send(OS, OR, xs.at[3], xr.at[3], nz[1])
     own_back = own_back + HR[...].astype(F32)
     cot = CC[mine].astype(F32)
-    SV[3:4, :] = column_sum(own_back * N2[...])
-    SV[4:5, :] = column_sum(own_back)
-    SV[5:6, :] = column_sum(cot)
+    EV[0, 1:2, :] = column_sum(own_back * N2[...])
+    EV[0, 2:3, :] = column_sum(own_back)
+    EV[0, 3:4, :] = column_sum(cot)
     dx1 = cot + norm_back(own_back, ln2_gain, N2[...], R2[...])
     DX1[...] = dx1
     branch = dx1.astype(BF16)
     GO[...] = branch
-    SV[2:3, :] = column_sum(branch.astype(F32))
+    EV[0, 0:1, :] = column_sum(branch.astype(F32))
     reduce_3(0)
     GOT[...] = GO[...].T
     DH1[...] = jnp.zeros(DH1.shape, F32)
 
     def attend_back(r):
-        da = dot_nn(GO[...], W[r, :, 512:768])[:, 64:256]
+        da = dot_nt(GO[...], W[r, 576:768, :])
         phi = PHI[r]
         dnum = da * INV[r]
         drest = -(dnum * ATT[r])
@@ -392,8 +439,12 @@
         back = back * COS[...] - swap_halves(back) * SIN[...]
         DQ[:, 0:384] = back.astype(BF16)
         DQ[:, 384:576] = dvalue.astype(BF16)
-        SV[6 + r:7 + r, 0:576] = column_sum(DQ[...].astype(F32))
-        DH1[...] += dot_nt(DQ[...], W[r, :, 0:576])
+        bias_sum = jnp.concatenate([column_sum(DQ[...].astype(F32)), jnp.zeros((1, 192), F32)], axis=1)
+        if r == 0:
+            LV[0, 2:3, :] = bias_sum
+        else:
+            EV[0, 5 + r:6 + r, :] = bias_sum
+        DH1[...] += dot_nn(DQ[...], qkv_rows_of(r))
 
     def store_attention(r):
         g = 4 + r
@@ -401,9 +452,34 @@
             cols = slice(n * 256, n * 256 + 256)
             G[g, :, :, :, cols] = dot_nn(H1T[...], DQ[:, cols]).astype(BF16).reshape(4, 2, 96, 256)
         edge = jnp.concatenate(
-            [dot_nn(H1T[...], DQ[:, 512:576]), dot_nn(GOT[...], AP[r, :, 64:256])], axis=1)
+            [dot_nn(H1T[...], DQ[:, 512:576]), dot_nn(GOT[...], AB[r])], axis=1)
         G[g, :, :, :, 512:768] = edge.astype(BF16).reshape(4, 2, 96, 256)
 
+    def small_1(V, k):
+        send(V.at[0], V.at[1], vs.at[k, 0], vr.at[k, 0], nc)
+
+    def small_2(V, k):
+        arrive(V.at[1], vr.at[k, 0])
+        V[2] = V[0] + V[1]
+        send(V.at[2], V.at[3], vs.at[k, 1], vr.at[k, 1], nx)
+
+    def small_3(V, k):
+        arrive(V.at[3], vr.at[k, 1])
+        V[4] = V[2] + V[3]
+        send(V.at[4], V.at[5], vs.at[k, 2], vr.at[k, 2], ny)
+
+    def small_4(V, k):
+        arrive(V.at[5], vr.at[k, 2])
+        V[6] = V[4] + V[5]
+        for r in (1, 2, 3):
+            send(V.at[6], V.at[6 + r], vs.at[k, 2 + r], vr.at[k, 2 + r], nz[r])
+
+    def small_5(V, k):
+        for r in (1, 2, 3):
+            arrive(V.at[6 + r], vr.at[k, 2 + r])
+
+    EV[0, 9:16, :] = jnp.zeros((7, 768), F32)
+    LV[0, 3:8, :] = jnp.zeros((5, 768), F32)
     attend_back(3)
     store_attention(3)
     reduce_1(7)
@@ -416,63 +492,72 @@
     reduce_3(2)
     reduce_4(1)
     attend_back(1)
+    small_1(EV, 0)
     store_attention(1)
     reduce_1(5)
     reduce_2(6)
     reduce_3(3)
     up_own = reduce_4(2)
     attend_back(0)
+    small_2(EV, 0)
     store_attention(0)
     reduce_1(4)
     reduce_2(5)
+
+    first_back = DH1[...]
+    LV[0, 0:1, :] = column_sum(first_back * N1[...])
+    LV[0, 1:2, :] = column_sum(first_back)
+    small_1(LV, 1)
+    reduce_2(4)
+    small_2(LV, 1)
+    reduce_3(7)
     reduce_4(3)
-    reduce_3(7)
-
-    first_back = DH1[...]
-    SV[0:1, :] = column_sum(first_back * N1[...])
-    SV[1:2, :] = column_sum(first_back)
-    send(SV, AR.at[0], vs.at[0], vr.at[0], nc)
     gx_ref[...] = (DX1[...] + norm_back(first_back, ln1_gain, N1[...], R1[...]))[0:live]
-    reduce_2(4)
-    arrive(AR.at[0], vr.at[0])
-    AR[1] = SV[...] + AR[0]
-    send(AR.at[1], AR.at[2], vs.at[1], vr.at[1], nx)
+    small_3(EV, 0)
+    reduce_3(6)
     reduce_4(7)
-    reduce_3(6)
-    gd_ref[...] = down_own + landed(1)
-    gu_ref[...] = up_own + landed(3)
+    small_3(LV, 1)
 
     output = dot_nn(ACT[0, mine], W[5]) + dot_nn(ACT[1, mine], W[7])
     arrive(OR, xr.at[3])
     output = X1[...] + output + OR[...].astype(F32) + b_down
     y_ref[...] = output[0:live].astype(BF16)
-
-    arrive(AR.at[2], vr.at[1])
-    AR[3] = AR[1] + AR[2]
-    send(AR.at[3], AR.at[4], vs.at[2], vr.at[2], ny)
+    small_4(EV, 0)
+    gd_ref[...] = down_own + landed(1)
+    gu_ref[...] = up_own + landed(3)
+
     reduce_3(5)
     reduce_4(6)
-    arrive(AR.at[4], vr.at[2])
-    AR[5] = AR[3] + AR[4]
-    for r in (1, 2, 3):
-        send(AR.at[5], AR.at[5 + r], vs.at[2 + r], vr.at[2 + r], nz[r])
+    small_4(LV, 1)
     reduce_3(4)
     reduce_4(5)
-    block = reduce_4(4)
-    for r in (1, 2, 3):
-        arrive(AR.at[5 + r], vr.at[2 + r])
-    sv_ref[0:6, :] = AR[5, 0:6, :] + AR[6, 0:6, :] + AR[7, 0:6, :] + AR[8, 0:6, :]
-    sv_ref[6:7, :] = AR[5, 10:11, :] + AR[7, 11:12, :]
-    bias = AR[5, 6:7, :] + AR[6, 7:8, :] + AR[7, 8:9, :] + AR[8, 9:10, :]
+    small_5(EV, 0)
+    small_5(LV, 1)
+    sv_ref[0:2, :] = LV[6, 0:2, :] + LV[7, 0:2, :] + LV[8, 0:2, :] + LV[9, 0:2, :]
+    sv_ref[2:6, :] = EV[6, 0:4, :] + EV[7, 0:4, :] + EV[8, 0:4, :] + EV[9, 0:4, :]
+    sv_ref[6:7, :] = EV[6, 4:5, :] + EV[8, 5:6, :]
+    bias = LV[6, 2:3, :] + EV[7, 6:7, :] + EV[8, 7:8, :] + EV[9, 8:9, :]
     bias = [bias[:, s * 192 + h * 64:s * 192 + h * 64 + 64] for h in range(3) for s in range(3)]
     sv_ref[7:8, :] = jnp.concatenate(bias + [jnp.zeros((1, 192), F32)], axis=1)
+    block = reduce_4(4)
     for r in (1, 2, 3):
         block = block + landed(4 + r)
     gq_ref[...] = jnp.concatenate(
         [block[:, s * 192 + h * 64:s * 192 + h * 64 + 64] for h in range(3) for s in range(3)], axis=1)
-    go_ref[...] = block[:, 576:768]
+    go_ref[...] = block[:, 576:768].T
     for copy in sends:
         copy.wait_send()
+    for condition, copy in late_sends:
+        pl.when(condition)(copy.wait_send)
+
+
+def write_outputs(y, gx, gq, go, gu, gd, sv, *outs):
+    refs = (y, gx, gq, go, gu, gd)
+    for source, target in zip(refs, outs[:6]):
+        target[...] = source[...]
+    for i, target in enumerate(outs[6:13]):
+        target[...] = sv[i:i + 1, :].reshape(768)
+    outs[13][...] = sv[7:8, 0:576].reshape(576)
 
 
 def trig_table(live, rows, head_dim):
@@ -490,10 +575,6 @@
 ):
     live, width = layer_input.shape
     rows = -(-live // 16) * 16
-    vectors = jnp.stack([
-        ln1_gain, ln1_bias, b_out, ln2_gain, ln2_bias, b_down, b_up,
-        jnp.pad(b_qkv, (0, width - b_qkv.shape[0])),
-    ])
     trig = jnp.asarray(trig_table(live, rows, features.shape[1]))
     vmem = pl.BlockSpec(memory_space=pltpu.VMEM)
     smem = pl.BlockSpec(memory_space=pltpu.SMEM)
@@ -512,12 +593,12 @@
             jax.ShapeDtypeStruct((live, width), BF16),
             jax.ShapeDtypeStruct((live, width), F32),
             jax.ShapeDtypeStruct((96, 576), F32),
-            jax.ShapeDtypeStruct((96, 192), F32),
+            jax.ShapeDtypeStruct((192, 96), F32),
             jax.ShapeDtypeStruct((96, 768), F32),
             jax.ShapeDtypeStruct((96, 768), F32),
             jax.ShapeDtypeStruct((8, 768), F32),
         ],
-        in_specs=[vmem, vmem, smem] + [vmem] * 5 + [anywhere] * 2,
+        in_specs=[vmem, vmem, smem] + [vmem] * 10 + [anywhere] * 4,
         out_specs=[vmem] * 7,
         scratch_shapes=[
             buf(8, 768, 768), wide(4, 80, 128), buf(2 * rows, 768), buf(2 * rows, 768),
@@ -526,21 +607,29 @@
             wide(rows, 768), wide(rows, 1), wide(rows, 768), wide(rows, 768),
             wide(rows, 384), wide(rows, 384), buf(4, 384, 192), buf(4, 384, 192),
             buf(4, rows, 192), wide(4, rows, 192), buf(4, rows, 192), wide(4, rows, 192),
-            wide(4, rows, 192), buf(4, rows, 256), wide(4, 192, 192), wide(4, 192, 192),
+            wide(4, rows, 192), buf(4, rows, 192), wide(4, 192, 192), wide(4, 192, 192),
             wide(2, 2 * rows, 768), buf(2, 2 * rows, 768), buf(2, 2 * rows, 768), buf(rows, 576),
             buf(rows, 768), buf(rows, 768), buf(rows, 768), buf(rows, 768),
             buf(8, 4, 2, 96, 768), buf(8, 4, 96, 768), buf(8, 2, 48, 768), buf(8, 2, 48, 768),
             buf(8, 2, 48, 768), buf(8, 2, 48, 768), buf(8, 96, 768), buf(8, 96, 768),
-            wide(9, 16, 768), wide(16, 768),
-            dma((2,)), dma((12,)), dma((12,)), dma((8, 8)), dma((8, 9)), dma((4,)), dma((4,)),
-            dma((8, 8)), dma((8, 8)), dma((6,)), dma((6,)),
+            wide(10, 16, 768), wide(10, 8, 768),
+            dma((4,)), dma((16,)), dma((8,)), dma((8, 8)), dma((8, 9)), dma((4,)), dma((4,)),
+            dma((8, 8)), dma((8, 8)), dma((2, 6)), dma((2, 6)),
         ],
         compiler_params=pltpu.CompilerParams(
             collective_id=0, has_side_effects=True, vmem_limit_bytes=67043328),
-    )(layer_input, cotangent, lengths, vectors, features, trig, w_qkv, w_out, w_up, w_down)
-    output, grad_x, qkv_piece, out_piece, up_piece, down_piece, small = outs
-    common, up_bias, qkv_bias = small[0:6], small[6], small[7, 0:576]
-    out_piece, down_piece = out_piece.T, down_piece.T
+    )(
+        layer_input, cotangent, lengths, ln1_gain, ln1_bias, b_out, ln2_gain, ln2_bias, b_down,
+        b_up, b_qkv, features.transpose(0, 2, 1), trig, w_qkv.T, w_out, w_up, w_down)
+    outs = pl.pallas_call(
+        write_outputs,
+        out_shape=[jax.ShapeDtypeStruct(out.shape, out.dtype) for out in outs[:6]]
+        + [jax.ShapeDtypeStruct((width,), F32)] * 7 + [jax.ShapeDtypeStruct((576,), F32)],
+        in_specs=[vmem] * 7,
+        out_specs=[vmem] * 14,
+    )(*outs)
+    output, grad_x, qkv_piece, out_piece, up_piece, down_piece, *common, up_bias, qkv_bias = outs
+    down_piece = down_piece.T
     if n_dp != GROUP:
         member = lax.axis_index("dp") % GROUP
 

time: 138 us -> 123 us (0.89)
  local copies, waits for them, and re-layouts: 19.4 us -> 0 us
  Pallas kernels: 117 us -> 121 us
    unnamed x16 -> x0, local copies, waits for them, and re-layouts: 10.1 us -> none
    another operation x9 -> x0, local copies, waits for them, and re-layouts: 5.48 us -> none  [local(): jnp.stack([ln1_gain, ln1_bias, b_out, ln2_gain, ln2_bias, b_down, b_up, j...]
    slice x2 -> x0, local copies, waits for them, and re-layouts: 3.08 us -> none  [the longest x1 1.67 us: local(): common[5]]
    pallas_call x0 -> x1, Pallas kernels: none -> 2.78 us  [local(): pl.pallas_call(write_outputs, out_shape=[jax.ShapeDtypeStruct(out.shape,...]
    pallas_call x1, Pallas kernels: 117 us -> 118 us  [local(): pl.pallas_call(functools.partial(layer_kernel, live), out_shape=[jax.Shap...]
where the time goes in v2:
time: 123 us; the launch traced here: 122 us
  Pallas kernels  121 us (98%)
    pallas_call x1, Pallas kernels, local(): pl.pallas_call(functools.partial(layer_kernel, live), out_shape=[jax.Shap...  118 us
    pallas_call x1, Pallas kernels, local(): pl.pallas_call(write_outputs, out_shape=[jax.ShapeDtypeStruct(out.shape,...  2.78 us

profile of v2, /device:TPU:0, one launch (start us, length us, event | category | flops | bytes accessed | tf_op | source)
XLA Modules:
  0.0 121.9 jit_solution(5927865575752584935)
XLA Ops:
  0.7 118.3 %shard_map.272 = (bf16[202,768]{1,0:T(8,128)(2,1)}, f32[202,768]{1,0:T(8,128)}, f32[96,576]{1,0:T(8,128)}, f32[192,96]{1,0:T(8,128)}, f32[96,768]{1,0:T(8,128)}, /*index=5*/f32[96,768]{1,0:T(8,128)}, f32[8,768]{1,0:T(8,128)}) custom-call(bf16[202,768]{1,0:T(8,128)(2,1)} %refs_0_.1, bf16[202,768]{1,0:T(8,128)(2,1)} %refs_1_.1, s32[4]{0:T(128)} %refs_2_.1, ...), custom_call_target="tpu_custom_call" | custom-call | tf_op jit(solution)/shard_map/pallas_call | solution.py:590
  118.9 2.8 %shard_map.273 = (bf16[202,768]{1,0:T(8,128)(2,1)}, f32[202,768]{1,0:T(8,128)}, f32[96,576]{1,0:T(8,128)}, f32[192,96]{1,0:T(8,128)}, f32[96,768]{1,0:T(8,128)},...) custom-call(bf16[202,768]{1,0:T(8,128)(2,1)} %get-tuple-element.35.y, ...), custom_call_target="tpu_custom_call" | custom-call | tf_op jit(solution)/shard_map/pallas_call | solution.py:624

commit v3 on v2

--- a/solution.py
+++ b/solution.py
@@ -64,7 +64,7 @@
         y_ref, gx_ref, gq_ref, go_ref, gu_ref, gd_ref, sv_ref,
         W, SP, CC, H2, CT, H2T, H1, H1T, GO, GOT, N1, R1, X1, N2, R2, DX1, DH1,
         COS, SIN, FH, FL, PHI, EE, VV, ATT, INV, AB, ST, TT, DA, ACT, DPRE, DQ,
-        OS, OR, HS, HR, G, Q0, QX, QY, T2, Q2, U, ZR, EV, LV,
+        OS, OR, HS, HR, G, Q0, QX, QY, T2, Q2, U, ZR, BL, EV, LV,
         local_sem, zs, zr, ags, agr, xs, xr, rs, rr, vs, vr,
     ) = refs
     rows = CC.shape[0] // 2
@@ -83,6 +83,12 @@
         return pl.multiple_of((yy * 4 + xx * 2 + cc) * 96, 96)
 
     sends = []
+    done = set()
+
+    def once(key, action, *args):
+        if key not in done:
+            done.add(key)
+            action(*args)
 
     def send(src, dst, send_sem, recv_sem, device):
         copy = pltpu.make_async_remote_copy(
@@ -152,8 +158,6 @@
             send_if(both, source, W.at[r, own], zs.at[r], agr.at[r, 0], nz[r])
     half = pl.ds(pl.multiple_of(c * 40, 8), 40)
     other_half = pl.ds(pl.multiple_of((1 - c) * 40, 8), 40)
-    for r in (1, 2, 3):
-        send(SP.at[0, half], SP.at[r, half], zs.at[8 + r], zr.at[r], nz[r])
 
     def forward(b, to_rank, slot):
         send_if(inner, W.at[b, own], W.at[slot, own], zs.at[3 + slot + to_rank], agr.at[slot, 0], nz[to_rank])
@@ -172,10 +176,12 @@
         send(W.at[b, own], W.at[b, own], ags.at[b, 1], agr.at[b, 2], ny)
         send(W.at[b, own], W.at[b, own], ags.at[b, 2], agr.at[b, 5], nc)
 
-    def gather_b(b):
+    def gather_x(b):
         arrive(W.at[b, at_x], agr.at[b, 1])
         send(W.at[b, at_x0], W.at[b, at_x0], ags.at[b, 3], agr.at[b, 3], ny)
         send(W.at[b, at_x], W.at[b, at_x], ags.at[b, 4], agr.at[b, 6], nc)
+
+    def gather_y(b):
         arrive(W.at[b, at_y], agr.at[b, 2])
         send(W.at[b, at_y1], W.at[b, at_y1], ags.at[b, 5], agr.at[b, 4], nx)
         send(W.at[b, at_y], W.at[b, at_y], ags.at[b, 6], agr.at[b, 7], nc)
@@ -201,6 +207,7 @@
             arrive(W.at[b, pl.ds(place(yy, xx, 1 - c), 96)], agr.at[b, 5 + k])
 
     rank = (0, 2, 0, 2, 0, 1, 2, 3)
+    kept = {0: gd_ref, 2: gu_ref, 4: BL}
 
     def reduce_1(g):
         send(G.at[g, :, 1 - c], Q0.at[g], rs.at[g, 0], rr.at[g, 0], nc)
@@ -230,10 +237,10 @@
         second = Q0[g, mine, 48:96].astype(F32) + QY[g, bx].astype(F32) + Q2[g, 1].astype(F32)
         total = jnp.concatenate([first, second], axis=0)
         if rank[g] == 0:
-            return total
-        U[g] = total.astype(BF16)
-        send(U.at[g], ZR.at[g], rs.at[g, 7], rr.at[g, 7], nz[rank[g]])
-        return None
+            kept[g][...] = total
+        else:
+            U[g] = total.astype(BF16)
+            send(U.at[g], ZR.at[g], rs.at[g, 7], rr.at[g, 7], nz[rank[g]])
 
     def landed(g):
         arrive(ZR.at[g], rr.at[g, 7])
@@ -300,57 +307,73 @@
         AB[r] = mixed
         X1[...] += dot_nn(mixed, W[r, 576:768, :])
 
-    gather_a(1)
-    forward(1, 3, 2)
-    for load in loads:
-        load.wait()
-    attend(0)
-    gather_a(second_rank)
-    forward(3, 1, 2)
-    send(wup_ref.at[own], W.at[6, own], zs.at[2], agr.at[6, 0], nz[2])
-    for r in (1, 2, 3):
-        gather_small(r)
-    gather_b(1)
-    gather_c(1)
-    gather_a(third_rank)
-    forward(2, 1, 3)
-    send(wdown_ref.at[own], W.at[7, own], zs.at[0], agr.at[7, 0], nz[2])
-    send(CC.at[0:rows], CC.at[rows:2 * rows], xs.at[0], xr.at[0], nz[1])
-    for r in (1, 2, 3):
-        small_done(r)
-    gather_d(1)
-    attend(1)
-    gather_b(second_rank)
-    gather_c(second_rank)
-    gather_a(6)
-    gather_d(second_rank)
-    attend(second_rank)
-    gather_b(third_rank)
-    gather_a(7)
-    gather_c(third_rank)
-    gather_d(third_rank)
-    attend(third_rank)
-
-    middle = X1[...] + b_out
-    X1[...] = middle
-    normed, factor = normalize(middle)
-    N2[...] = normed
-    R2[...] = factor
-    second = (normed * ln2_gain + ln2_bias).astype(BF16)
-    H2[0:rows, :] = second
-    send(H2.at[0:rows], H2.at[rows:2 * rows], xs.at[1], xr.at[1], nz[1])
-
-    gather_b(6)
-    gather_c(6)
-    gather_b(7)
-    gather_d(6)
-    arrive(CC.at[rows:2 * rows], xr.at[0])
+    theirs = pl.ds(rows, rows)
+    mine_rows = pl.ds(0, rows)
     up = (4, 6)
     down = (5, 7)
-    DA[0] = dot_nt(CC[...], W[5])
-    gather_c(7)
+    EV[0, 9:16, :] = jnp.zeros((7, 768), F32)
+    LV[0, 3:8, :] = jnp.zeros((5, 768), F32)
+
+    def share_small():
+        for r in (1, 2, 3):
+            send(SP.at[0, half], SP.at[r, half], zs.at[8 + r], zr.at[r], nz[r])
+
+    def share_up():
+        send(wup_ref.at[own], W.at[6, own], zs.at[2], agr.at[6, 0], nz[2])
+
+    def share_down():
+        send(wdown_ref.at[own], W.at[7, own], zs.at[0], agr.at[7, 0], nz[2])
+
+    def share_cotangent():
+        send(CC.at[0:rows], CC.at[rows:2 * rows], xs.at[0], xr.at[0], nz[1])
+
+    def whole(b):
+        for r in (2, 3) if b is second_rank or b is third_rank else (1,) if b == 1 else (2,):
+            once(("small", r), small_done, r)
+        gather_d(b)
+
+    def loaded(i):
+        once(("load", i), loads[i].wait)
+
+    def cotangent_here():
+        once("cotangent", arrive, CC.at[rows:2 * rows], xr.at[0])
+
+    def second_here():
+        once("second", arrive, H2.at[rows:2 * rows], xr.at[1])
+
+    def attend_first():
+        loaded(0)
+        loaded(1)
+        attend(0)
+
+    def attend_next(b):
+        whole(b)
+        attend(b)
+
+    def second_norm():
+        middle = X1[...] + b_out
+        X1[...] = middle
+        normed, factor = normalize(middle)
+        N2[...] = normed
+        R2[...] = factor
+        H2[0:rows, :] = (normed * ln2_gain + ln2_bias).astype(BF16)
+        send(H2.at[0:rows], H2.at[rows:2 * rows], xs.at[1], xr.at[1], nz[1])
+
+    def back_hidden(q):
+        cotangent_here()
+        if q == 0:
+            loaded(3)
+        else:
+            gather_d(7)
+        DA[q] = dot_nt(CC[...], W[down[q]])
 
     def feed(q, s):
+        if s == 1:
+            second_here()
+        if q == 0:
+            loaded(2)
+        else:
+            once("up", whole, 6)
         part = pl.ds(s * rows, rows)
         bias = jnp.concatenate([SP[2 * q, 72 + i:73 + i, :] for i in range(6)], axis=1)
         pre = dot_nn(H2[part], W[up[q]]) + bias
@@ -359,59 +382,62 @@
         slope = half + pre * jnp.exp(-0.5 * pre * pre) * (0.5 / np.pi) ** 0.5
         DPRE[q, part] = (DA[q, part] * slope).astype(BF16)
 
-    feed(0, 0)
-    gather_d(7)
-    DA[1] = dot_nt(CC[...], W[7])
-    feed(1, 0)
-    CT[...] = CC[...].T
-    H1T[...] = H1[...].T
-    arrive(H2.at[rows:2 * rows], xr.at[1])
-    theirs = pl.ds(rows, rows)
-    mine = pl.ds(0, rows)
-
-    def store_block(g, left, right):
+    def transpose_rows():
+        cotangent_here()
+        CT[...] = CC[...].T
+        H1T[...] = H1[...].T
+
+    def transpose_second():
+        H2T[...] = H2[...].T
+
+    def store_block(g):
+        q = g % 2
+        if g >= 2:
+            once("turned", transpose_second)
         for n in range(3):
             cols = slice(n * 256, n * 256 + 256)
-            G[g, :, :, :, cols] = dot_nn(left, right[:, cols]).astype(BF16).reshape(4, 2, 96, 256)
-
-    feed(0, 1)
-    store_block(0, CT[...], ACT[0])
-    reduce_1(0)
-    feed(1, 1)
-    HS[...] = (dot_nt(DPRE[0, theirs], W[4]) + dot_nt(DPRE[1, theirs], W[6])).astype(BF16)
-    send(HS, HR, xs.at[2], xr.at[2], nz[1])
-
-    store_block(1, CT[...], ACT[1])
-    reduce_1(1)
-    reduce_2(0)
-    H2T[...] = H2[...].T
-    store_block(2, H2T[...], DPRE[0])
-    reduce_1(2)
-    reduce_2(1)
-    store_block(3, H2T[...], DPRE[1])
-    reduce_1(3)
-    reduce_2(2)
-    OS[...] = (dot_nn(ACT[0, theirs], W[5]) + dot_nn(ACT[1, theirs], W[7])).astype(BF16)
-    for q in range(2):
-        EV[0, 4 + q:5 + q, :] = column_sum(DPRE[q].astype(F32))
-    own_back = dot_nt(DPRE[0, mine], W[4]) + dot_nt(DPRE[1, mine], W[6])
-    reduce_2(3)
-
-    arrive(HR, xr.at[2])
-    send(OS, OR, xs.at[3], xr.at[3], nz[1])
-    own_back = own_back + HR[...].astype(F32)
-    cot = CC[mine].astype(F32)
-    EV[0, 1:2, :] = column_sum(own_back * N2[...])
-    EV[0, 2:3, :] = column_sum(own_back)
-    EV[0, 3:4, :] = column_sum(cot)
-    dx1 = cot + norm_back(own_back, ln2_gain, N2[...], R2[...])
-    DX1[...] = dx1
-    branch = dx1.astype(BF16)
-    GO[...] = branch
-    EV[0, 0:1, :] = column_sum(branch.astype(F32))
-    reduce_3(0)
-    GOT[...] = GO[...].T
-    DH1[...] = jnp.zeros(DH1.shape, F32)
+            if g < 2:
+                block = dot_nn(CT[...], ACT[q, :, cols])
+            else:
+                block = dot_nn(H2T[...], DPRE[q, :, cols])
+            G[g, :, :, :, cols] = block.astype(BF16).reshape(4, 2, 96, 256)
+        reduce_1(g)
+
+    def hidden_back():
+        HS[...] = (dot_nt(DPRE[0, theirs], W[4]) + dot_nt(DPRE[1, theirs], W[6])).astype(BF16)
+        send(HS, HR, xs.at[2], xr.at[2], nz[1])
+
+    def hidden_out():
+        OS[...] = (dot_nn(ACT[0, theirs], W[5]) + dot_nn(ACT[1, theirs], W[7])).astype(BF16)
+        send(OS, OR, xs.at[3], xr.at[3], nz[1])
+        for q in range(2):
+            EV[0, 4 + q:5 + q, :] = column_sum(DPRE[q].astype(F32))
+
+    def own_hidden_back():
+        DH1[...] = dot_nt(DPRE[0, mine_rows], W[4]) + dot_nt(DPRE[1, mine_rows], W[6])
+
+    def second_norm_back():
+        arrive(HR, xr.at[2])
+        own_back = DH1[...] + HR[...].astype(F32)
+        cot = CC[mine_rows].astype(F32)
+        EV[0, 1:2, :] = column_sum(own_back * N2[...])
+        EV[0, 2:3, :] = column_sum(own_back)
+        EV[0, 3:4, :] = column_sum(cot)
+        dx1 = cot + norm_back(own_back, ln2_gain, N2[...], R2[...])
+        DX1[...] = dx1
+        branch = dx1.astype(BF16)
+        GO[...] = branch
+        EV[0, 0:1, :] = column_sum(branch.astype(F32))
+        GOT[...] = GO[...].T
+
+    def store_attention(r):
+        g = 4 + r
+        for n in range(2):
+            cols = slice(n * 256, n * 256 + 256)
+            G[g, :, :, :, cols] = dot_nn(H1T[...], DQ[:, cols]).astype(BF16).reshape(4, 2, 96, 256)
+        edge = jnp.concatenate(
+            [dot_nn(H1T[...], DQ[:, 512:576]), dot_nn(GOT[...], AB[r])], axis=1)
+        G[g, :, :, :, 512:768] = edge.astype(BF16).reshape(4, 2, 96, 256)
 
     def attend_back(r):
         da = dot_nt(GO[...], W[r, 576:768, :])
@@ -444,16 +470,14 @@
             LV[0, 2:3, :] = bias_sum
         else:
             EV[0, 5 + r:6 + r, :] = bias_sum
-        DH1[...] += dot_nn(DQ[...], qkv_rows_of(r))
-
-    def store_attention(r):
-        g = 4 + r
-        for n in range(2):
-            cols = slice(n * 256, n * 256 + 256)
-            G[g, :, :, :, cols] = dot_nn(H1T[...], DQ[:, cols]).astype(BF16).reshape(4, 2, 96, 256)
-        edge = jnp.concatenate(
-            [dot_nn(H1T[...], DQ[:, 512:576]), dot_nn(GOT[...], AB[r])], axis=1)
-        G[g, :, :, :, 512:768] = edge.astype(BF16).reshape(4, 2, 96, 256)
+        grad = dot_nn(DQ[...], qkv_rows_of(r))
+        if "back" in done:
+            DH1[...] += grad
+        else:
+            DH1[...] = grad
+        done.add("back")
+        store_attention(r)
+        reduce_1(4 + r)
 
     def small_1(V, k):
         send(V.at[0], V.at[1], vs.at[k, 0], vr.at[k, 0], nc)
@@ -478,73 +502,135 @@
         for r in (1, 2, 3):
             arrive(V.at[6 + r], vr.at[k, 2 + r])
 
-    EV[0, 9:16, :] = jnp.zeros((7, 768), F32)
-    LV[0, 3:8, :] = jnp.zeros((5, 768), F32)
+    def first_norm_sums():
+        first_back = DH1[...]
+        LV[0, 0:1, :] = column_sum(first_back * N1[...])
+        LV[0, 1:2, :] = column_sum(first_back)
+        small_1(LV, 1)
+
+    def input_grad():
+        gx_ref[...] = (DX1[...] + norm_back(DH1[...], ln1_gain, N1[...], R1[...]))[0:live]
+
+    def layer_output():
+        output = dot_nn(ACT[0, mine_rows], W[5]) + dot_nn(ACT[1, mine_rows], W[7])
+        arrive(OR, xr.at[3])
+        output = X1[...] + output + OR[...].astype(F32) + b_down
+        y_ref[...] = output[0:live].astype(BF16)
+
+    def down_done():
+        gd_ref[...] += landed(1)
+
+    def up_done():
+        gu_ref[...] += landed(3)
+
+    def attention_done():
+        block = BL[...]
+        for r in (1, 2, 3):
+            block = block + landed(4 + r)
+        gq_ref[...] = jnp.concatenate(
+            [block[:, s * 192 + h * 64:s * 192 + h * 64 + 64] for h in range(3) for s in range(3)], axis=1)
+        go_ref[...] = block[:, 576:768].T
+
+    share_small()
+    gather_a(1)
+    forward(1, 3, 2)
+    gather_a(second_rank)
+    share_down()
+    forward(3, 1, 2)
+    gather_y(1)
+    gather_x(1)
+    gather_a(third_rank)
+    forward(2, 1, 3)
+    gather_small(3)
+    gather_x(second_rank)
+    gather_c(1)
+    share_up()
+    gather_small(1)
+    gather_y(second_rank)
+    attend_first()
+    share_cotangent()
+    gather_y(third_rank)
+    gather_x(third_rank)
+    gather_small(2)
+    gather_a(7)
+    attend_next(1)
+    gather_c(second_rank)
+    attend_next(second_rank)
+    gather_a(6)
+    gather_c(third_rank)
+    attend_next(third_rank)
+    second_norm()
+    gather_x(7)
+    gather_y(7)
+    back_hidden(0)
+    gather_x(6)
+    gather_y(6)
+    gather_c(7)
+    back_hidden(1)
+    feed(0, 0)
+    transpose_rows()
+    gather_c(6)
+    feed(1, 0)
+    feed(1, 1)
+    feed(0, 1)
+    hidden_back()
+    store_block(3)
+    store_block(1)
+    reduce_2(3)
+    reduce_2(1)
+    hidden_out()
+    reduce_3(3)
+    store_block(0)
+    store_block(2)
+    own_hidden_back()
+    second_norm_back()
+    reduce_3(1)
+    reduce_2(2)
+    attend_back(2)
+    reduce_4(3)
+    attend_back(1)
+    reduce_2(6)
+    reduce_2(5)
+    reduce_4(1)
     attend_back(3)
-    store_attention(3)
-    reduce_1(7)
-    reduce_3(1)
-    down_own = reduce_4(0)
-    attend_back(2)
-    store_attention(2)
-    reduce_1(6)
+    small_1(EV, 0)
+    reduce_3(6)
+    small_2(EV, 0)
+    attend_back(0)
     reduce_2(7)
+    reduce_4(6)
+    first_norm_sums()
+    small_3(EV, 0)
     reduce_3(2)
-    reduce_4(1)
-    attend_back(1)
-    small_1(EV, 0)
-    store_attention(1)
-    reduce_1(5)
-    reduce_2(6)
-    reduce_3(3)
-    up_own = reduce_4(2)
-    attend_back(0)
-    small_2(EV, 0)
-    store_attention(0)
-    reduce_1(4)
-    reduce_2(5)
-
-    first_back = DH1[...]
-    LV[0, 0:1, :] = column_sum(first_back * N1[...])
-    LV[0, 1:2, :] = column_sum(first_back)
-    small_1(LV, 1)
+    reduce_3(5)
+    reduce_3(7)
+    small_2(LV, 1)
+    reduce_2(0)
+    layer_output()
+    small_4(EV, 0)
     reduce_2(4)
-    small_2(LV, 1)
-    reduce_3(7)
-    reduce_4(3)
-    gx_ref[...] = (DX1[...] + norm_back(first_back, ln1_gain, N1[...], R1[...]))[0:live]
-    small_3(EV, 0)
-    reduce_3(6)
+    reduce_4(5)
+    reduce_4(2)
     reduce_4(7)
     small_3(LV, 1)
-
-    output = dot_nn(ACT[0, mine], W[5]) + dot_nn(ACT[1, mine], W[7])
-    arrive(OR, xr.at[3])
-    output = X1[...] + output + OR[...].astype(F32) + b_down
-    y_ref[...] = output[0:live].astype(BF16)
-    small_4(EV, 0)
-    gd_ref[...] = down_own + landed(1)
-    gu_ref[...] = up_own + landed(3)
-
-    reduce_3(5)
-    reduce_4(6)
+    small_5(EV, 0)
+    reduce_3(0)
+    reduce_3(4)
     small_4(LV, 1)
-    reduce_3(4)
-    reduce_4(5)
-    small_5(EV, 0)
+    reduce_4(4)
+    reduce_4(0)
+    attention_done()
+    up_done()
+    input_grad()
+    down_done()
     small_5(LV, 1)
+
     sv_ref[0:2, :] = LV[6, 0:2, :] + LV[7, 0:2, :] + LV[8, 0:2, :] + LV[9, 0:2, :]
     sv_ref[2:6, :] = EV[6, 0:4, :] + EV[7, 0:4, :] + EV[8, 0:4, :] + EV[9, 0:4, :]
     sv_ref[6:7, :] = EV[6, 4:5, :] + EV[8, 5:6, :]
     bias = LV[6, 2:3, :] + EV[7, 6:7, :] + EV[8, 7:8, :] + EV[9, 8:9, :]
     bias = [bias[:, s * 192 + h * 64:s * 192 + h * 64 + 64] for h in range(3) for s in range(3)]
     sv_ref[7:8, :] = jnp.concatenate(bias + [jnp.zeros((1, 192), F32)], axis=1)
-    block = reduce_4(4)
-    for r in (1, 2, 3):
-        block = block + landed(4 + r)
-    gq_ref[...] = jnp.concatenate(
-        [block[:, s * 192 + h * 64:s * 192 + h * 64 + 64] for h in range(3) for s in range(3)], axis=1)
-    go_ref[...] = block[:, 576:768].T
     for copy in sends:
         copy.wait_send()
     for condition, copy in late_sends:
@@ -611,7 +697,7 @@
             wide(2, 2 * rows, 768), buf(2, 2 * rows, 768), buf(2, 2 * rows, 768), buf(rows, 576),
             buf(rows, 768), buf(rows, 768), buf(rows, 768), buf(rows, 768),
             buf(8, 4, 2, 96, 768), buf(8, 4, 96, 768), buf(8, 2, 48, 768), buf(8, 2, 48, 768),
-            buf(8, 2, 48, 768), buf(8, 2, 48, 768), buf(8, 96, 768), buf(8, 96, 768),
+            buf(8, 2, 48, 768), buf(8, 2, 48, 768), buf(8, 96, 768), buf(8, 96, 768), wide(96, 768),
             wide(10, 16, 768), wide(10, 8, 768),
             dma((4,)), dma((16,)), dma((8,)), dma((8, 8)), dma((8, 9)), dma((4,)), dma((4,)),
             dma((8, 8)), dma((8, 8)), dma((2, 6)), dma((2, 6)),

time: 123 us -> 104 us (0.85); the launches traced: 122 us -> 104 us
  Pallas kernels: 121 us -> 103 us
    pallas_call x1, Pallas kernels: 118 us -> 101 us  [local(): pl.pallas_call(functools.partial(layer_kernel, live), out_shape=[jax.Shap...]
where the time goes in v3:
time: 104 us
  Pallas kernels  103 us (99%)
    pallas_call x1, Pallas kernels, local(): pl.pallas_call(functools.partial(layer_kernel, live), out_shape=[jax.Shap...  101 us
    pallas_call x1, Pallas kernels, local(): pl.pallas_call(write_outputs, out_shape=[jax.ShapeDtypeStruct(out.shape,...  2.78 us

profile of v3, /device:TPU:0, one launch (start us, length us, event | category | flops | bytes accessed | tf_op | source)
XLA Modules:
  0.0 104.2 jit_solution(17056726810289043174)
XLA Ops:
  0.7 100.6 %shard_map.272 = (bf16[202,768]{1,0:T(8,128)(2,1)}, f32[202,768]{1,0:T(8,128)}, f32[96,576]{1,0:T(8,128)}, f32[192,96]{1,0:T(8,128)}, f32[96,768]{1,0:T(8,128)}, /*index=5*/f32[96,768]{1,0:T(8,128)}, f32[8,768]{1,0:T(8,128)}) custom-call(bf16[202,768]{1,0:T(8,128)(2,1)} %refs_0_.1, bf16[202,768]{1,0:T(8,128)(2,1)} %refs_1_.1, s32[4]{0:T(128)} %refs_2_.1, ...), custom_call_target="tpu_custom_call" | custom-call | tf_op jit(solution)/shard_map/pallas_call | solution.py:676
  101.3 2.8 %shard_map.273 = (bf16[202,768]{1,0:T(8,128)(2,1)}, f32[202,768]{1,0:T(8,128)}, f32[96,576]{1,0:T(8,128)}, f32[192,96]{1,0:T(8,128)}, f32[96,768]{1,0:T(8,128)},...) custom-call(bf16[202,768]{1,0:T(8,128)(2,1)} %get-tuple-element.35.y, ...), custom_call_target="tpu_custom_call" | custom-call | tf_op jit(solution)/shard_map/pallas_call | solution.py:710

commit v4 on v3

--- a/solution.py
+++ b/solution.py
@@ -153,43 +153,60 @@
     out_rows = pl.ds(pl.multiple_of(jnp.maximum(own.start - 576, 0), 96), 96)
     qkv_rows = pl.ds(pl.multiple_of(jnp.minimum(own.start, 480), 96), 96)
     for r, condition in ((1, None), (3, inner)):
-        for part, source in ((in_qkv, wqkv_ref.at[qkv_rows]), (jnp.logical_not(in_qkv), wout_ref.at[out_rows])):
-            both = part if condition is None else jnp.logical_and(part, condition)
-            send_if(both, source, W.at[r, own], zs.at[r], agr.at[r, 0], nz[r])
+        for h in (0, 1):
+            here = pl.ds(pl.multiple_of(own.start + 48 * h, 48), 48)
+            for part, ref, start in ((in_qkv, wqkv_ref, qkv_rows.start), (jnp.logical_not(in_qkv), wout_ref, out_rows.start)):
+                both = part if condition is None else jnp.logical_and(part, condition)
+                source = ref.at[pl.ds(pl.multiple_of(start + 48 * h, 48), 48)]
+                send_if(both, source, W.at[r, here], zs.at[r + 16 * h], agr.at[r, h], nz[r])
     half = pl.ds(pl.multiple_of(c * 40, 8), 40)
     other_half = pl.ds(pl.multiple_of((1 - c) * 40, 8), 40)
 
-    def forward(b, to_rank, slot):
-        send_if(inner, W.at[b, own], W.at[slot, own], zs.at[3 + slot + to_rank], agr.at[slot, 0], nz[to_rank])
-
-    at_x = pl.ds(place(by, 1 - bx, c), 96)
-    at_y = pl.ds(place(1 - by, bx, c), 96)
+    def forward(b, to_rank, slot, h):
+        here = pl.ds(pl.multiple_of(own.start + 48 * h, 48), 48)
+        send_if(inner, W.at[b, here], W.at[slot, here], zs.at[3 + slot + to_rank + 16 * h], agr.at[slot, h], nz[to_rank])
+
     at_d = pl.ds(place(1 - by, 1 - bx, c), 96)
     at_x0 = pl.ds(place(by, 1 - bx, c), 48)
     at_y1 = pl.ds(pl.multiple_of(place(1 - by, bx, c) + 48, 48), 48)
     at_d0 = pl.ds(place(1 - by, 1 - bx, c), 48)
     at_d1 = pl.ds(pl.multiple_of(place(1 - by, 1 - bx, c) + 48, 48), 48)
 
-    def gather_a(b):
-        arrive(W.at[b, own], agr.at[b, 0])
-        send(W.at[b, own], W.at[b, own], ags.at[b, 0], agr.at[b, 1], nx)
-        send(W.at[b, own], W.at[b, own], ags.at[b, 1], agr.at[b, 2], ny)
-        send(W.at[b, own], W.at[b, own], ags.at[b, 2], agr.at[b, 5], nc)
-
-    def gather_x(b):
-        arrive(W.at[b, at_x], agr.at[b, 1])
-        send(W.at[b, at_x0], W.at[b, at_x0], ags.at[b, 3], agr.at[b, 3], ny)
-        send(W.at[b, at_x], W.at[b, at_x], ags.at[b, 4], agr.at[b, 6], nc)
-
-    def gather_y(b):
-        arrive(W.at[b, at_y], agr.at[b, 2])
-        send(W.at[b, at_y1], W.at[b, at_y1], ags.at[b, 5], agr.at[b, 4], nx)
-        send(W.at[b, at_y], W.at[b, at_y], ags.at[b, 6], agr.at[b, 7], nc)
+    def rows_at(yy, xx, cc, h):
+        start = place(yy, xx, cc)
+        return pl.ds(start, 96) if h is None else pl.ds(pl.multiple_of(start + 48 * h, 48), 48)
+
+    def halves(b):
+        return (None,) if isinstance(b, int) and b > 1 else (0, 1)
+
+    def gather_a(b, h=None):
+        k = h or 0
+        part = W.at[b, rows_at(by, bx, c, h)]
+        arrive(part, agr.at[b, k])
+        send(part, part, ags.at[b, k], agr.at[b, 2 + k], nx)
+        send(part, part, ags.at[b, 2 + k], agr.at[b, 4 + k], ny)
+        send(part, part, ags.at[b, 4 + k], agr.at[b, 6 + k], nc)
+
+    def gather_x(b, h=None):
+        k = h or 0
+        part = W.at[b, rows_at(by, 1 - bx, c, h)]
+        arrive(part, agr.at[b, 2 + k])
+        if h != 1:
+            send(W.at[b, at_x0], W.at[b, at_x0], ags.at[b, 6], agr.at[b, 14], ny)
+        send(part, part, ags.at[b, 8 + k], agr.at[b, 8 + k], nc)
+
+    def gather_y(b, h=None):
+        k = h or 0
+        part = W.at[b, rows_at(1 - by, bx, c, h)]
+        arrive(part, agr.at[b, 4 + k])
+        if h != 0:
+            send(W.at[b, at_y1], W.at[b, at_y1], ags.at[b, 7], agr.at[b, 15], nx)
+        send(part, part, ags.at[b, 10 + k], agr.at[b, 10 + k], nc)
 
     def gather_c(b):
-        arrive(W.at[b, at_d0], agr.at[b, 3])
-        arrive(W.at[b, at_d1], agr.at[b, 4])
-        send(W.at[b, at_d], W.at[b, at_d], ags.at[b, 7], agr.at[b, 8], nc)
+        arrive(W.at[b, at_d0], agr.at[b, 14])
+        arrive(W.at[b, at_d1], agr.at[b, 15])
+        send(W.at[b, at_d], W.at[b, at_d], ags.at[b, 12], agr.at[b, 12], nc)
 
     def gather_small(r):
         arrive(SP.at[r, half], zr.at[r])
@@ -203,8 +220,10 @@
             [W[r, h * 192 + s * 64:h * 192 + s * 64 + 64, :] for s in range(3) for h in range(3)], axis=0)
 
     def gather_d(b):
-        for k, (yy, xx) in enumerate(((by, bx), (by, 1 - bx), (1 - by, bx), (1 - by, 1 - bx))):
-            arrive(W.at[b, pl.ds(place(yy, xx, 1 - c), 96)], agr.at[b, 5 + k])
+        for n, (yy, xx) in enumerate(((by, bx), (by, 1 - bx), (1 - by, bx))):
+            for h in halves(b):
+                arrive(W.at[b, rows_at(yy, xx, 1 - c, h)], agr.at[b, 6 + 2 * n + (h or 0)])
+        arrive(W.at[b, rows_at(1 - by, 1 - bx, 1 - c, None)], agr.at[b, 12])
 
     rank = (0, 2, 0, 2, 0, 1, 2, 3)
     kept = {0: gd_ref, 2: gu_ref, 4: BL}
@@ -338,8 +357,11 @@
     def cotangent_here():
         once("cotangent", arrive, CC.at[rows:2 * rows], xr.at[0])
 
-    def second_here():
-        once("second", arrive, H2.at[rows:2 * rows], xr.at[1])
+    cuts = ((0, 96), (96, rows))
+
+    def second_here(k):
+        lo, hi = cuts[k]
+        once(("second", k), arrive, H2.at[rows + lo:rows + hi], xr.at[1 + 3 * k])
 
     def attend_first():
         loaded(0)
@@ -350,14 +372,15 @@
         whole(b)
         attend(b)
 
-    def second_norm():
-        middle = X1[...] + b_out
-        X1[...] = middle
+    def second_norm(k):
+        lo, hi = cuts[k]
+        middle = X1[lo:hi] + b_out
+        X1[lo:hi] = middle
         normed, factor = normalize(middle)
-        N2[...] = normed
-        R2[...] = factor
-        H2[0:rows, :] = (normed * ln2_gain + ln2_bias).astype(BF16)
-        send(H2.at[0:rows], H2.at[rows:2 * rows], xs.at[1], xr.at[1], nz[1])
+        N2[lo:hi] = normed
+        R2[lo:hi] = factor
+        H2[lo:hi, :] = (normed * ln2_gain + ln2_bias).astype(BF16)
+        send(H2.at[lo:hi], H2.at[rows + lo:rows + hi], xs.at[1 + 3 * k], xr.at[1 + 3 * k], nz[1])
 
     def back_hidden(q):
         cotangent_here()
@@ -367,14 +390,16 @@
             gather_d(7)
         DA[q] = dot_nt(CC[...], W[down[q]])
 
-    def feed(q, s):
-        if s == 1:
-            second_here()
+    def feed(q, k=None):
+        lo, hi = 0, rows
+        if k is not None:
+            second_here(k)
+            lo, hi = rows + cuts[k][0], rows + cuts[k][1]
         if q == 0:
             loaded(2)
         else:
             once("up", whole, 6)
-        part = pl.ds(s * rows, rows)
+        part = pl.ds(lo, hi - lo)
         bias = jnp.concatenate([SP[2 * q, 72 + i:73 + i, :] for i in range(6)], axis=1)
         pre = dot_nn(H2[part], W[up[q]]) + bias
         half = 0.5 * (1.0 + lax.erf(pre * (0.5 ** 0.5)))
@@ -403,9 +428,11 @@
             G[g, :, :, :, cols] = block.astype(BF16).reshape(4, 2, 96, 256)
         reduce_1(g)
 
-    def hidden_back():
-        HS[...] = (dot_nt(DPRE[0, theirs], W[4]) + dot_nt(DPRE[1, theirs], W[6])).astype(BF16)
-        send(HS, HR, xs.at[2], xr.at[2], nz[1])
+    def hidden_back(k):
+        lo, hi = cuts[k]
+        part = pl.ds(rows + lo, hi - lo)
+        HS[lo:hi] = (dot_nt(DPRE[0, part], W[4]) + dot_nt(DPRE[1, part], W[6])).astype(BF16)
+        send(HS.at[lo:hi], HR.at[lo:hi], xs.at[2 + 3 * k], xr.at[2 + 3 * k], nz[1])
 
     def hidden_out():
         OS[...] = (dot_nn(ACT[0, theirs], W[5]) + dot_nn(ACT[1, theirs], W[7])).astype(BF16)
@@ -417,7 +444,8 @@
         DH1[...] = dot_nt(DPRE[0, mine_rows], W[4]) + dot_nt(DPRE[1, mine_rows], W[6])
 
     def second_norm_back():
-        arrive(HR, xr.at[2])
+        for k, (lo, hi) in enumerate(cuts):
+            arrive(HR.at[lo:hi], xr.at[2 + 3 * k])
         own_back = DH1[...] + HR[...].astype(F32)
         cot = CC[mine_rows].astype(F32)
         EV[0, 1:2, :] = column_sum(own_back * N2[...])
@@ -531,98 +559,114 @@
             [block[:, s * 192 + h * 64:s * 192 + h * 64 + 64] for h in range(3) for s in range(3)], axis=1)
         go_ref[...] = block[:, 576:768].T
 
+    gather_a(1, 0)
+    forward(1, 3, 2, 0)
+    gather_a(second_rank, 0)
+    forward(3, 1, 2, 0)
+    gather_a(1, 1)
+    forward(1, 3, 2, 1)
+    share_down()
+    gather_a(second_rank, 1)
+    forward(3, 1, 2, 1)
+    gather_x(1, 0)
+    gather_y(1, 0)
+    gather_a(third_rank, 0)
+    forward(2, 1, 3, 0)
+    gather_y(1, 1)
+    gather_a(third_rank, 1)
+    forward(2, 1, 3, 1)
     share_small()
-    gather_a(1)
-    forward(1, 3, 2)
-    gather_a(second_rank)
-    share_down()
-    forward(3, 1, 2)
-    gather_y(1)
-    gather_x(1)
-    gather_a(third_rank)
-    forward(2, 1, 3)
+    attend_first()
+    gather_x(second_rank, 0)
+    gather_x(1, 1)
+    share_up()
+    gather_x(third_rank, 0)
+    gather_y(third_rank, 0)
+    gather_y(second_rank, 0)
+    gather_y(second_rank, 1)
+    gather_y(third_rank, 1)
+    gather_a(7)
+    gather_small(1)
+    gather_x(second_rank, 1)
+    gather_x(third_rank, 1)
+    gather_small(2)
+    gather_c(1)
     gather_small(3)
-    gather_x(second_rank)
-    gather_c(1)
-    share_up()
-    gather_small(1)
-    gather_y(second_rank)
-    attend_first()
     share_cotangent()
-    gather_y(third_rank)
-    gather_x(third_rank)
-    gather_small(2)
-    gather_a(7)
+    gather_c(second_rank)
     attend_next(1)
-    gather_c(second_rank)
     attend_next(second_rank)
     gather_a(6)
     gather_c(third_rank)
     attend_next(third_rank)
-    second_norm()
+    gather_y(7)
+    second_norm(0)
     gather_x(7)
-    gather_y(7)
+    second_norm(1)
+    gather_y(6)
+    gather_x(6)
     back_hidden(0)
-    gather_x(6)
-    gather_y(6)
+    feed(0)
     gather_c(7)
+    transpose_rows()
+    feed(0, 0)
+    gather_c(6)
     back_hidden(1)
-    feed(0, 0)
-    transpose_rows()
-    gather_c(6)
+    feed(1)
     feed(1, 0)
+    hidden_back(0)
     feed(1, 1)
-    feed(0, 1)
-    hidden_back()
     store_block(3)
     store_block(1)
+    feed(0, 1)
+    hidden_back(1)
     reduce_2(3)
+    own_hidden_back()
     reduce_2(1)
+    store_block(2)
     hidden_out()
     reduce_3(3)
+    reduce_2(2)
+    second_norm_back()
+    attend_back(2)
+    reduce_3(1)
+    reduce_4(3)
+    attend_back(3)
+    reduce_2(6)
+    attend_back(1)
+    reduce_2(7)
+    reduce_4(1)
+    small_1(EV, 0)
     store_block(0)
-    store_block(2)
-    own_hidden_back()
-    second_norm_back()
-    reduce_3(1)
-    reduce_2(2)
-    attend_back(2)
-    reduce_4(3)
-    attend_back(1)
-    reduce_2(6)
-    reduce_2(5)
-    reduce_4(1)
-    attend_back(3)
-    small_1(EV, 0)
     reduce_3(6)
     small_2(EV, 0)
     attend_back(0)
-    reduce_2(7)
+    reduce_2(5)
     reduce_4(6)
+    small_3(EV, 0)
     first_norm_sums()
-    small_3(EV, 0)
-    reduce_3(2)
+    reduce_3(7)
     reduce_3(5)
-    reduce_3(7)
+    reduce_2(4)
     small_2(LV, 1)
     reduce_2(0)
     layer_output()
     small_4(EV, 0)
-    reduce_2(4)
     reduce_4(5)
-    reduce_4(2)
+    reduce_3(2)
+    input_grad()
     reduce_4(7)
     small_3(LV, 1)
-    small_5(EV, 0)
     reduce_3(0)
     reduce_3(4)
     small_4(LV, 1)
     reduce_4(4)
     reduce_4(0)
+    reduce_4(2)
+    small_5(EV, 0)
+    down_done()
+    up_done()
     attention_done()
-    up_done()
-    input_grad()
-    down_done()
     small_5(LV, 1)
 
     sv_ref[0:2, :] = LV[6, 0:2, :] + LV[7, 0:2, :] + LV[8, 0:2, :] + LV[9, 0:2, :]
@@ -699,7 +743,7 @@
             buf(8, 4, 2, 96, 768), buf(8, 4, 96, 768), buf(8, 2, 48, 768), buf(8, 2, 48, 768),
             buf(8, 2, 48, 768), buf(8, 2, 48, 768), buf(8, 96, 768), buf(8, 96, 768), wide(96, 768),
             wide(10, 16, 768), wide(10, 8, 768),
-            dma((4,)), dma((16,)), dma((8,)), dma((8, 8)), dma((8, 9)), dma((4,)), dma((4,)),
+            dma((4,)), dma((32,)), dma((8,)), dma((8, 16)), dma((8, 16)), dma((6,)), dma((6,)),
             dma((8, 8)), dma((8, 8)), dma((2, 6)), dma((2, 6)),
         ],
         compiler_params=pltpu.CompilerParams(

time: 104 us -> 101 us (0.971)
  Pallas kernels: 103 us -> 100 us
    pallas_call x1, Pallas kernels: 101 us -> 97.6 us  [local(): pl.pallas_call(functools.partial(layer_kernel, live), out_shape=[jax.Shap...]
where the time goes in v4:
time: 101 us
  Pallas kernels  100 us (99%)
    pallas_call x1, Pallas kernels, local(): pl.pallas_call(functools.partial(layer_kernel, live), out_shape=[jax.Shap...  97.6 us
    pallas_call x1, Pallas kernels, local(): pl.pallas_call(write_outputs, out_shape=[jax.ShapeDtypeStruct(out.shape,...  2.78 us

profile of v4, /device:TPU:0, one launch (start us, length us, event | category | flops | bytes accessed | tf_op | source)
XLA Modules:
  0.0 101.2 jit_solution(9009220475118799438)
XLA Ops:
  0.7 97.6 %shard_map.272 = (bf16[202,768]{1,0:T(8,128)(2,1)}, f32[202,768]{1,0:T(8,128)}, f32[96,576]{1,0:T(8,128)}, f32[192,96]{1,0:T(8,128)}, f32[96,768]{1,0:T(8,128)}, /*index=5*/f32[96,768]{1,0:T(8,128)}, f32[8,768]{1,0:T(8,128)}) custom-call(bf16[202,768]{1,0:T(8,128)(2,1)} %refs_0_.1, bf16[202,768]{1,0:T(8,128)(2,1)} %refs_1_.1, s32[4]{0:T(128)} %refs_2_.1, ...), custom_call_target="tpu_custom_call" | custom-call | tf_op jit(solution)/shard_map/pallas_call | solution.py:720
  98.2 2.8 %shard_map.273 = (bf16[202,768]{1,0:T(8,128)(2,1)}, f32[202,768]{1,0:T(8,128)}, f32[96,576]{1,0:T(8,128)}, f32[192,96]{1,0:T(8,128)}, f32[96,768]{1,0:T(8,128)},...) custom-call(bf16[202,768]{1,0:T(8,128)(2,1)} %get-tuple-element.35.y, ...), custom_call_target="tpu_custom_call" | custom-call | tf_op jit(solution)/shard_map/pallas_call | solution.py:754

commit v5 on v4

--- a/solution.py
+++ b/solution.py
@@ -59,14 +59,15 @@
 
 def layer_kernel(live, *refs):
     (
+        wqkv_ref, wout_ref, wup_ref, wdown_ref,
         x_ref, c_ref, len_ref, ln1_gain_ref, ln1_bias_ref, b_out_ref, ln2_gain_ref, ln2_bias_ref,
-        b_down_ref, b_up_ref, b_qkv_ref, feat_ref, trig_ref, wqkv_ref, wout_ref, wup_ref, wdown_ref,
+        b_down_ref, b_up_ref, b_qkv_ref, feat_ref, trig_ref,
         y_ref, gx_ref, gq_ref, go_ref, gu_ref, gd_ref, sv_ref,
         W, SP, CC, H2, CT, H2T, H1, H1T, GO, GOT, N1, R1, X1, N2, R2, DX1, DH1,
         COS, SIN, FH, FL, PHI, EE, VV, ATT, INV, AB, ST, TT, DA, ACT, DPRE, DQ,
         OS, OR, HS, HR, G, Q0, QX, QY, T2, Q2, U, ZR, BL, EV, LV,
-        local_sem, zs, zr, ags, agr, xs, xr, rs, rr, vs, vr,
-    ) = refs
+        local_sem, in_sem, out_sem, zs, zr, ags, agr, xs, xr, rs, rr, vs, vr,
+    ) = refs[13:17] + refs[24:]
     rows = CC.shape[0] // 2
     dp = lax.axis_index("dp")
     z = lax.axis_index("mp")
@@ -108,6 +109,19 @@
     for device in (nx, ny, nc, nz[1], nz[2], nz[3]):
         pl.semaphore_signal(barrier, inc=1, device_id=device, device_id_type=MESH)
 
+    takes = [
+        pltpu.make_async_copy(source, target, in_sem.at[i])
+        for i, (source, target) in enumerate(zip(refs[:13], refs[24:37]))
+    ]
+    for take in takes:
+        take.start()
+    gives = []
+
+    def give(i):
+        copy = pltpu.make_async_copy(refs[37 + i], refs[17 + i], out_sem.at[i])
+        copy.start()
+        gives.append(copy)
+
     loads = [
         pltpu.make_async_copy(source, target, local_sem.at[i])
         for i, (source, target) in enumerate((
@@ -116,18 +130,6 @@
     ]
     for load in loads:
         load.start()
-
-    SP[0, 0:64, 0:96] = feat_ref[...].reshape(96, 64).T
-    qkv_bias = b_qkv_ref[...].reshape(1, 576)
-    qkv_bias = jnp.concatenate(
-        [qkv_bias[:, h * 192 + s * 64:h * 192 + s * 64 + 64] for s in range(3) for h in range(3)]
-        + [jnp.zeros((1, 64), F32)], axis=1)
-    for i in range(5):
-        SP[0, 64 + i:65 + i, :] = qkv_bias[:, i * 128:i * 128 + 128]
-    up_bias = b_up_ref[...].reshape(1, 768)
-    for i in range(6):
-        SP[0, 72 + i:73 + i, :] = up_bias[:, i * 128:i * 128 + 128]
-    CC[0:rows, :] = jnp.concatenate([c_ref[...].astype(F32), jnp.zeros((rows - live, 768), F32)], axis=0).astype(BF16)
 
     pl.semaphore_wait(barrier, 6)
 
@@ -161,6 +163,20 @@
                 send_if(both, source, W.at[r, here], zs.at[r + 16 * h], agr.at[r, h], nz[r])
     half = pl.ds(pl.multiple_of(c * 40, 8), 40)
     other_half = pl.ds(pl.multiple_of((1 - c) * 40, 8), 40)
+
+    for take in takes:
+        take.wait()
+    SP[0, 0:64, 0:96] = feat_ref[...].reshape(96, 64).T
+    qkv_bias = b_qkv_ref[...].reshape(1, 576)
+    qkv_bias = jnp.concatenate(
+        [qkv_bias[:, h * 192 + s * 64:h * 192 + s * 64 + 64] for s in range(3) for h in range(3)]
+        + [jnp.zeros((1, 64), F32)], axis=1)
+    for i in range(5):
+        SP[0, 64 + i:65 + i, :] = qkv_bias[:, i * 128:i * 128 + 128]
+    up_bias = b_up_ref[...].reshape(1, 768)
+    for i in range(6):
+        SP[0, 72 + i:73 + i, :] = up_bias[:, i * 128:i * 128 + 128]
+    CC[0:rows, :] = jnp.concatenate([c_ref[...].astype(F32), jnp.zeros((rows - live, 768), F32)], axis=0).astype(BF16)
 
     def forward(b, to_rank, slot, h):
         here = pl.ds(pl.multiple_of(own.start + 48 * h, 48), 48)
@@ -538,18 +554,22 @@
 
     def input_grad():
         gx_ref[...] = (DX1[...] + norm_back(DH1[...], ln1_gain, N1[...], R1[...]))[0:live]
+        give(1)
 
     def layer_output():
         output = dot_nn(ACT[0, mine_rows], W[5]) + dot_nn(ACT[1, mine_rows], W[7])
         arrive(OR, xr.at[3])
         output = X1[...] + output + OR[...].astype(F32) + b_down
         y_ref[...] = output[0:live].astype(BF16)
+        give(0)
 
     def down_done():
         gd_ref[...] += landed(1)
+        give(5)
 
     def up_done():
         gu_ref[...] += landed(3)
+        give(4)
 
     def attention_done():
         block = BL[...]
@@ -557,7 +577,9 @@
             block = block + landed(4 + r)
         gq_ref[...] = jnp.concatenate(
             [block[:, s * 192 + h * 64:s * 192 + h * 64 + 64] for h in range(3) for s in range(3)], axis=1)
+        give(2)
         go_ref[...] = block[:, 576:768].T
+        give(3)
 
     gather_a(1, 0)
     forward(1, 3, 2, 0)
@@ -675,10 +697,13 @@
     bias = LV[6, 2:3, :] + EV[7, 6:7, :] + EV[8, 7:8, :] + EV[9, 8:9, :]
     bias = [bias[:, s * 192 + h * 64:s * 192 + h * 64 + 64] for h in range(3) for s in range(3)]
     sv_ref[7:8, :] = jnp.concatenate(bias + [jnp.zeros((1, 192), F32)], axis=1)
+    give(6)
     for copy in sends:
         copy.wait_send()
     for condition, copy in late_sends:
         pl.when(condition)(copy.wait_send)
+    for copy in gives:
+        copy.wait()
 
 
 def write_outputs(y, gx, gq, go, gu, gd, sv, *outs):
@@ -707,7 +732,6 @@
     rows = -(-live // 16) * 16
     trig = jnp.asarray(trig_table(live, rows, features.shape[1]))
     vmem = pl.BlockSpec(memory_space=pltpu.VMEM)
-    smem = pl.BlockSpec(memory_space=pltpu.SMEM)
     anywhere = pl.BlockSpec(memory_space=pl.ANY)
     dma = pltpu.SemaphoreType.DMA
 
@@ -728,9 +752,14 @@
             jax.ShapeDtypeStruct((96, 768), F32),
             jax.ShapeDtypeStruct((8, 768), F32),
         ],
-        in_specs=[vmem, vmem, smem] + [vmem] * 10 + [anywhere] * 4,
-        out_specs=[vmem] * 7,
+        in_specs=[anywhere] * 17,
+        out_specs=[anywhere] * 7,
         scratch_shapes=[
+            buf(live, width), buf(live, width), pltpu.SMEM(lengths.shape, jnp.int32)] + [
+            wide(width) for _ in range(6)] + [
+            wide(*b_up.shape), wide(*b_qkv.shape), wide(features.shape[0], features.shape[2], features.shape[1]),
+            wide(*trig.shape), buf(live, width), wide(live, width), wide(96, 576), wide(192, 96),
+            wide(96, 768), wide(96, 768), wide(8, 768),
             buf(8, 768, 768), wide(4, 80, 128), buf(2 * rows, 768), buf(2 * rows, 768),
             buf(768, 2 * rows), buf(768, 2 * rows), buf(rows, 768), buf(768, rows),
             buf(rows, 768), buf(768, rows), wide(rows, 768), wide(rows, 1), wide(rows, 768),
@@ -743,7 +772,7 @@
             buf(8, 4, 2, 96, 768), buf(8, 4, 96, 768), buf(8, 2, 48, 768), buf(8, 2, 48, 768),
             buf(8, 2, 48, 768), buf(8, 2, 48, 768), buf(8, 96, 768), buf(8, 96, 768), wide(96, 768),
             wide(10, 16, 768), wide(10, 8, 768),
-            dma((4,)), dma((32,)), dma((8,)), dma((8, 16)), dma((8, 16)), dma((6,)), dma((6,)),
+            dma((4,)), dma((13,)), dma((7,)), dma((32,)), dma((8,)), dma((8, 16)), dma((8, 16)), dma((6,)), dma((6,)),
             dma((8, 8)), dma((8, 8)), dma((2, 6)), dma((2, 6)),
         ],
         compiler_params=pltpu.CompilerParams(

time: 101 us -> 99.3 us (0.983)
  Pallas kernels: 100 us -> 98.4 us
    pallas_call x1, Pallas kernels: 97.6 us -> 95.6 us  [local(): pl.pallas_call(functools.partial(layer_kernel, live), out_shape=[jax.Shap...]
where the time goes in v5:
time: 99.3 us; the launch traced here: 99.2 us
  Pallas kernels  98.4 us (99%)
    pallas_call x1, Pallas kernels, local(): pl.pallas_call(functools.partial(layer_kernel, live), out_shape=[jax.Shap...  95.6 us
    pallas_call x1, Pallas kernels, local(): pl.pallas_call(write_outputs, out_shape=[jax.ShapeDtypeStruct(out.shape,...  2.78 us

profile of v5, /device:TPU:0, one launch (start us, length us, event | category | flops | bytes accessed | tf_op | source)
XLA Modules:
  0.0 99.2 jit_solution(7136332447537588734)
XLA Ops:
  0.7 95.6 %shard_map.272 = (bf16[202,768]{1,0:T(8,128)(2,1)}, f32[202,768]{1,0:T(8,128)}, f32[96,576]{1,0:T(8,128)}, f32[192,96]{1,0:T(8,128)}, f32[96,768]{1,0:T(8,128)}, /*index=5*/f32[96,768]{1,0:T(8,128)}, f32[8,768]{1,0:T(8,128)}) custom-call(bf16[202,768]{1,0:T(8,128)(2,1)} %refs_0_.1, bf16[202,768]{1,0:T(8,128)(2,1)} %refs_1_.1, s32[4]{0:T(128)} %refs_2_.1, ...), custom_call_target="tpu_custom_call" | custom-call | tf_op jit(solution)/shard_map/pallas_call | solution.py:744
  96.3 2.8 %shard_map.273 = (bf16[202,768]{1,0:T(8,128)(2,1)}, f32[202,768]{1,0:T(8,128)}, f32[96,576]{1,0:T(8,128)}, f32[192,96]{1,0:T(8,128)}, f32[96,768]{1,0:T(8,128)},...) custom-call(bf16[202,768]{1,0:T(8,128)(2,1)} %get-tuple-element.35.y, ...), custom_call_target="tpu_custom_call" | custom-call | tf_op jit(solution)/shard_map/pallas_call | solution.py:783

commit v6 on v5

--- a/solution.py
+++ b/solution.py
@@ -65,7 +65,7 @@
         y_ref, gx_ref, gq_ref, go_ref, gu_ref, gd_ref, sv_ref,
         W, SP, CC, H2, CT, H2T, H1, H1T, GO, GOT, N1, R1, X1, N2, R2, DX1, DH1,
         COS, SIN, FH, FL, PHI, EE, VV, ATT, INV, AB, ST, TT, DA, ACT, DPRE, DQ,
-        OS, OR, HS, HR, G, Q0, QX, QY, T2, Q2, U, ZR, BL, EV, LV,
+        OS, OR, HS, HR, G, Q0, QX, QY, T2, Q2, U, ZR, VS, VR, BL, EV, LV,
         local_sem, in_sem, out_sem, zs, zr, ags, agr, xs, xr, rs, rr, vs, vr,
     ) = refs[13:17] + refs[24:]
     rows = CC.shape[0] // 2
@@ -275,7 +275,24 @@
             kept[g][...] = total
         else:
             U[g] = total.astype(BF16)
-            send(U.at[g], ZR.at[g], rs.at[g, 7], rr.at[g, 7], nz[rank[g]])
+            if g < 4:
+                send(U.at[g], ZR.at[g], rs.at[g, 7], rr.at[g, 7], nz[rank[g]])
+            else:
+                send_if(jnp.logical_not(inner), U.at[g], ZR.at[g], rs.at[g, 7], rr.at[g, 7], nz[1])
+
+    def chain(g):
+        source, landing, target, there, device = {
+            7: (ZR.at[6], rr.at[6, 7], VR.at[0], rr.at[4, 7], nz[3]),
+            6: (ZR.at[7], rr.at[7, 7], VR.at[1], rr.at[0, 7], nz[3]),
+            5: (VR.at[1], rr.at[0, 7], ZR.at[5], rr.at[5, 7], nz[1]),
+        }[g]
+
+        @pl.when(inner)
+        def _():
+            arrive(source, landing)
+            VS[g - 5] = (source[...].astype(F32) + U[g].astype(F32)).astype(BF16)
+
+        send_if(inner, VS.at[g - 5], target, rs.at[g, 7], there, device)
 
     def landed(g):
         arrive(ZR.at[g], rr.at[g, 7])
@@ -572,124 +589,130 @@
         give(4)
 
     def attention_done():
-        block = BL[...]
-        for r in (1, 2, 3):
-            block = block + landed(4 + r)
+        @pl.when(inner)
+        def _():
+            arrive(VR.at[0], rr.at[4, 7])
+            BL[...] += VR[0].astype(F32)
+
+        block = BL[...] + landed(5)
         gq_ref[...] = jnp.concatenate(
             [block[:, s * 192 + h * 64:s * 192 + h * 64 + 64] for h in range(3) for s in range(3)], axis=1)
         give(2)
         go_ref[...] = block[:, 576:768].T
         give(3)
 
+    share_small()
     gather_a(1, 0)
     forward(1, 3, 2, 0)
     gather_a(second_rank, 0)
     forward(3, 1, 2, 0)
+    gather_a(second_rank, 1)
+    forward(3, 1, 2, 1)
     gather_a(1, 1)
     forward(1, 3, 2, 1)
     share_down()
-    gather_a(second_rank, 1)
-    forward(3, 1, 2, 1)
-    gather_x(1, 0)
-    gather_y(1, 0)
     gather_a(third_rank, 0)
     forward(2, 1, 3, 0)
-    gather_y(1, 1)
+    gather_y(second_rank, 1)
+    share_up()
+    gather_x(second_rank, 0)
+    gather_small(1)
     gather_a(third_rank, 1)
     forward(2, 1, 3, 1)
-    share_small()
+    gather_x(1, 0)
+    gather_y(1, 1)
     attend_first()
-    gather_x(second_rank, 0)
+    gather_y(second_rank, 0)
+    share_cotangent()
+    gather_small(3)
+    gather_x(second_rank, 1)
     gather_x(1, 1)
-    share_up()
+    gather_c(second_rank)
+    gather_y(1, 0)
     gather_x(third_rank, 0)
+    gather_y(third_rank, 1)
+    gather_small(2)
     gather_y(third_rank, 0)
-    gather_y(second_rank, 0)
-    gather_y(second_rank, 1)
-    gather_y(third_rank, 1)
     gather_a(7)
-    gather_small(1)
-    gather_x(second_rank, 1)
     gather_x(third_rank, 1)
-    gather_small(2)
     gather_c(1)
-    gather_small(3)
-    share_cotangent()
-    gather_c(second_rank)
-    attend_next(1)
     attend_next(second_rank)
     gather_a(6)
     gather_c(third_rank)
+    attend_next(1)
     attend_next(third_rank)
+    second_norm(0)
+    second_norm(1)
     gather_y(7)
-    second_norm(0)
     gather_x(7)
-    second_norm(1)
     gather_y(6)
     gather_x(6)
     back_hidden(0)
+    gather_c(7)
+    back_hidden(1)
+    transpose_rows()
+    gather_c(6)
     feed(0)
-    gather_c(7)
-    transpose_rows()
     feed(0, 0)
-    gather_c(6)
-    back_hidden(1)
     feed(1)
     feed(1, 0)
     hidden_back(0)
     feed(1, 1)
-    store_block(3)
     store_block(1)
     feed(0, 1)
+    reduce_2(1)
     hidden_back(1)
+    store_block(3)
+    store_block(2)
+    own_hidden_back()
     reduce_2(3)
-    own_hidden_back()
-    reduce_2(1)
-    store_block(2)
     hidden_out()
-    reduce_3(3)
+    reduce_3(1)
     reduce_2(2)
     second_norm_back()
+    attend_back(3)
     attend_back(2)
-    reduce_3(1)
+    reduce_4(1)
+    reduce_3(3)
+    reduce_2(7)
+    attend_back(1)
+    small_1(EV, 0)
+    small_2(EV, 0)
+    reduce_2(6)
+    attend_back(0)
     reduce_4(3)
-    attend_back(3)
-    reduce_2(6)
-    attend_back(1)
-    reduce_2(7)
-    reduce_4(1)
-    small_1(EV, 0)
+    reduce_3(7)
+    first_norm_sums()
+    small_2(LV, 1)
     store_block(0)
+    small_3(EV, 0)
+    reduce_2(5)
     reduce_3(6)
-    small_2(EV, 0)
-    attend_back(0)
-    reduce_2(5)
-    reduce_4(6)
-    small_3(EV, 0)
-    first_norm_sums()
-    reduce_3(7)
-    reduce_3(5)
-    reduce_2(4)
-    small_2(LV, 1)
-    reduce_2(0)
-    layer_output()
-    small_4(EV, 0)
-    reduce_4(5)
-    reduce_3(2)
-    input_grad()
     reduce_4(7)
     small_3(LV, 1)
+    small_4(EV, 0)
+    reduce_2(4)
+    reduce_3(5)
+    reduce_4(6)
+    input_grad()
+    chain(6)
+    layer_output()
+    reduce_2(0)
+    small_4(LV, 1)
+    reduce_4(5)
+    small_5(EV, 0)
+    reduce_3(4)
+    chain(7)
+    reduce_3(2)
+    chain(5)
     reduce_3(0)
-    reduce_3(4)
-    small_4(LV, 1)
+    reduce_4(2)
     reduce_4(4)
+    up_done()
+    small_5(LV, 1)
+    attention_done()
     reduce_4(0)
-    reduce_4(2)
-    small_5(EV, 0)
     down_done()
-    up_done()
-    attention_done()
-    small_5(LV, 1)
 
     sv_ref[0:2, :] = LV[6, 0:2, :] + LV[7, 0:2, :] + LV[8, 0:2, :] + LV[9, 0:2, :]
     sv_ref[2:6, :] = EV[6, 0:4, :] + EV[7, 0:4, :] + EV[8, 0:4, :] + EV[9, 0:4, :]
@@ -770,7 +793,7 @@
             wide(2, 2 * rows, 768), buf(2, 2 * rows, 768), buf(2, 2 * rows, 768), buf(rows, 576),
             buf(rows, 768), buf(rows, 768), buf(rows, 768), buf(rows, 768),
             buf(8, 4, 2, 96, 768), buf(8, 4, 96, 768), buf(8, 2, 48, 768), buf(8, 2, 48, 768),
-            buf(8, 2, 48, 768), buf(8, 2, 48, 768), buf(8, 96, 768), buf(8, 96, 768), wide(96, 768),
+            buf(8, 2, 48, 768), buf(8, 2, 48, 768), buf(8, 96, 768), buf(8, 96, 768), buf(3, 96, 768), buf(2, 96, 768), wide(96, 768),
             wide(10, 16, 768), wide(10, 8, 768),
             dma((4,)), dma((13,)), dma((7,)), dma((32,)), dma((8,)), dma((8, 16)), dma((8, 16)), dma((6,)), dma((6,)),
             dma((8, 8)), dma((8, 8)), dma((2, 6)), dma((2, 6)),

time: 99.3 us -> 98.2 us (0.989)
  Pallas kernels: 98.4 us -> 97.2 us
    pallas_call x1, Pallas kernels: 95.6 us -> 94.4 us  [local(): pl.pallas_call(functools.partial(layer_kernel, live), out_shape=[jax.Shap...]
where the time goes in v6:
time: 98.2 us; the launch traced here: 98 us
  Pallas kernels  97.2 us (99%)
    pallas_call x1, Pallas kernels, local(): pl.pallas_call(functools.partial(layer_kernel, live), out_shape=[jax.Shap...  94.4 us
    pallas_call x1, Pallas kernels, local(): pl.pallas_call(write_outputs, out_shape=[jax.ShapeDtypeStruct(out.shape,...  2.78 us

profile of v6, /device:TPU:0, one launch (start us, length us, event | category | flops | bytes accessed | tf_op | source)
XLA Modules:
  0.0 98.0 jit_solution(6024336649599301483)
XLA Ops:
  0.7 94.4 %shard_map.272 = (bf16[202,768]{1,0:T(8,128)(2,1)}, f32[202,768]{1,0:T(8,128)}, f32[96,576]{1,0:T(8,128)}, f32[192,96]{1,0:T(8,128)}, f32[96,768]{1,0:T(8,128)}, /*index=5*/f32[96,768]{1,0:T(8,128)}, f32[8,768]{1,0:T(8,128)}) custom-call(bf16[202,768]{1,0:T(8,128)(2,1)} %refs_0_.1, bf16[202,768]{1,0:T(8,128)(2,1)} %refs_1_.1, s32[4]{0:T(128)} %refs_2_.1, ...), custom_call_target="tpu_custom_call" | custom-call | tf_op jit(solution)/shard_map/pallas_call | solution.py:767
  95.0 2.8 %shard_map.273 = (bf16[202,768]{1,0:T(8,128)(2,1)}, f32[202,768]{1,0:T(8,128)}, f32[96,576]{1,0:T(8,128)}, f32[192,96]{1,0:T(8,128)}, f32[96,768]{1,0:T(8,128)},...) custom-call(bf16[202,768]{1,0:T(8,128)(2,1)} %get-tuple-element.35.y, ...), custom_call_target="tpu_custom_call" | custom-call | tf_op jit(solution)/shard_map/pallas_call | solution.py:806

commit v7 on v6

--- a/solution.py
+++ b/solution.py
@@ -601,118 +601,118 @@
         go_ref[...] = block[:, 576:768].T
         give(3)
 
-    share_small()
+    gather_a(second_rank, 0)
+    forward(3, 1, 2, 0)
     gather_a(1, 0)
     forward(1, 3, 2, 0)
-    gather_a(second_rank, 0)
-    forward(3, 1, 2, 0)
-    gather_a(second_rank, 1)
-    forward(3, 1, 2, 1)
     gather_a(1, 1)
     forward(1, 3, 2, 1)
     share_down()
+    gather_a(second_rank, 1)
+    forward(3, 1, 2, 1)
     gather_a(third_rank, 0)
     forward(2, 1, 3, 0)
-    gather_y(second_rank, 1)
-    share_up()
-    gather_x(second_rank, 0)
-    gather_small(1)
+    gather_y(1, 1)
+    gather_y(second_rank, 0)
+    gather_x(1, 0)
+    share_small()
+    gather_x(1, 1)
     gather_a(third_rank, 1)
     forward(2, 1, 3, 1)
-    gather_x(1, 0)
-    gather_y(1, 1)
+    gather_x(second_rank, 0)
+    gather_y(1, 0)
+    gather_y(second_rank, 1)
+    gather_x(third_rank, 0)
+    share_up()
+    gather_small(1)
+    gather_x(second_rank, 1)
     attend_first()
-    gather_y(second_rank, 0)
+    gather_y(third_rank, 1)
+    gather_c(1)
+    gather_x(third_rank, 1)
+    gather_small(3)
+    gather_a(7)
+    gather_y(third_rank, 0)
+    gather_small(2)
     share_cotangent()
-    gather_small(3)
-    gather_x(second_rank, 1)
-    gather_x(1, 1)
+    attend_next(1)
     gather_c(second_rank)
-    gather_y(1, 0)
-    gather_x(third_rank, 0)
-    gather_y(third_rank, 1)
-    gather_small(2)
-    gather_y(third_rank, 0)
-    gather_a(7)
-    gather_x(third_rank, 1)
-    gather_c(1)
+    gather_c(third_rank)
+    gather_a(6)
     attend_next(second_rank)
-    gather_a(6)
-    gather_c(third_rank)
-    attend_next(1)
     attend_next(third_rank)
     second_norm(0)
+    gather_x(7)
+    gather_y(7)
     second_norm(1)
-    gather_y(7)
-    gather_x(7)
     gather_y(6)
+    transpose_rows()
     gather_x(6)
     back_hidden(0)
+    feed(0)
     gather_c(7)
+    gather_c(6)
     back_hidden(1)
-    transpose_rows()
-    gather_c(6)
-    feed(0)
     feed(0, 0)
     feed(1)
     feed(1, 0)
     hidden_back(0)
     feed(1, 1)
-    store_block(1)
+    store_block(3)
     feed(0, 1)
-    reduce_2(1)
     hidden_back(1)
-    store_block(3)
-    store_block(2)
     own_hidden_back()
     reduce_2(3)
+    store_block(1)
+    store_block(2)
+    reduce_2(1)
+    reduce_2(2)
+    store_block(0)
     hidden_out()
-    reduce_3(1)
-    reduce_2(2)
     second_norm_back()
     attend_back(3)
+    reduce_3(1)
+    reduce_3(3)
     attend_back(2)
+    reduce_2(7)
     reduce_4(1)
-    reduce_3(3)
-    reduce_2(7)
-    attend_back(1)
-    small_1(EV, 0)
-    small_2(EV, 0)
     reduce_2(6)
     attend_back(0)
+    reduce_3(2)
+    attend_back(1)
+    first_norm_sums()
+    small_1(EV, 0)
     reduce_4(3)
+    small_2(LV, 1)
     reduce_3(7)
-    first_norm_sums()
-    small_2(LV, 1)
-    store_block(0)
+    small_2(EV, 0)
+    reduce_3(6)
+    small_3(LV, 1)
+    reduce_2(5)
+    reduce_4(7)
     small_3(EV, 0)
-    reduce_2(5)
-    reduce_3(6)
-    reduce_4(7)
-    small_3(LV, 1)
+    reduce_2(0)
+    input_grad()
+    small_4(LV, 1)
+    reduce_4(6)
+    chain(6)
+    reduce_3(5)
     small_4(EV, 0)
     reduce_2(4)
-    reduce_3(5)
-    reduce_4(6)
-    input_grad()
-    chain(6)
+    reduce_4(5)
+    reduce_4(2)
     layer_output()
-    reduce_2(0)
-    small_4(LV, 1)
-    reduce_4(5)
-    small_5(EV, 0)
+    small_5(LV, 1)
+    reduce_3(0)
+    up_done()
+    chain(5)
+    chain(7)
     reduce_3(4)
-    chain(7)
-    reduce_3(2)
-    chain(5)
-    reduce_3(0)
-    reduce_4(2)
-    reduce_4(4)
-    up_done()
-    small_5(LV, 1)
-    attention_done()
     reduce_4(0)
     down_done()
+    small_5(EV, 0)
+    reduce_4(4)
+    attention_done()
 
     sv_ref[0:2, :] = LV[6, 0:2, :] + LV[7, 0:2, :] + LV[8, 0:2, :] + LV[9, 0:2, :]
     sv_ref[2:6, :] = EV[6, 0:4, :] + EV[7, 0:4, :] + EV[8, 0:4, :] + EV[9, 0:4, :]

time: 98.2 us -> 97.2 us (0.990)
  Pallas kernels: 97.2 us -> 96.2 us
where the time goes in v7:
time: 97.2 us; the launch traced here: 97 us
  Pallas kernels  96.2 us (99%)
    pallas_call x1, Pallas kernels, local(): pl.pallas_call(functools.partial(layer_kernel, live), out_shape=[jax.Shap...  93.4 us
    pallas_call x1, Pallas kernels, local(): pl.pallas_call(write_outputs, out_shape=[jax.ShapeDtypeStruct(out.shape,...  2.78 us

profile of v7, /device:TPU:0, one launch (start us, length us, event | category | flops | bytes accessed | tf_op | source)
XLA Modules:
  0.0 97.0 jit_solution(74822255029566558)
XLA Ops:
  0.7 93.4 %shard_map.272 = (bf16[202,768]{1,0:T(8,128)(2,1)}, f32[202,768]{1,0:T(8,128)}, f32[96,576]{1,0:T(8,128)}, f32[192,96]{1,0:T(8,128)}, f32[96,768]{1,0:T(8,128)}, /*index=5*/f32[96,768]{1,0:T(8,128)}, f32[8,768]{1,0:T(8,128)}) custom-call(bf16[202,768]{1,0:T(8,128)(2,1)} %refs_0_.1, bf16[202,768]{1,0:T(8,128)(2,1)} %refs_1_.1, s32[4]{0:T(128)} %refs_2_.1, ...), custom_call_target="tpu_custom_call" | custom-call | tf_op jit(solution)/shard_map/pallas_call | solution.py:767
  94.1 2.8 %shard_map.273 = (bf16[202,768]{1,0:T(8,128)(2,1)}, f32[202,768]{1,0:T(8,128)}, f32[96,576]{1,0:T(8,128)}, f32[192,96]{1,0:T(8,128)}, f32[96,768]{1,0:T(8,128)},...) custom-call(bf16[202,768]{1,0:T(8,128)(2,1)} %get-tuple-element.35.y, ...), custom_call_target="tpu_custom_call" | custom-call | tf_op jit(solution)/shard_map/pallas_call | solution.py:806
